TPU v7x, 256 devices: a whole 4x4x8 slice. The times are simulated.
256 devices in a mesh: domain: 16 (over z, y_lo), band: 16 (over x, y_hi, core).
Axes of the slice: x: 4, y: 4 (y_hi: 2, y_lo: 2; y = y_hi * 2 + y_lo), z: 8, core: 2. Of those that a mesh axis runs over, the one named last changes fastest.
Arguments:
- states: float32 [19584, 2048], P('domain', 'band'), may hold values from -6 to 6
- potential: float32 [19584], P('domain'), may hold values from -1 to 1
- node_mass: float32 [19584], P('domain'), may hold values from 0.3 to 3
- cell_matrix: bfloat16 [729, 729], replicated, as said below
- connectivity: int32 [32, 729], P('domain'), may hold values from 0 to 1376, as said below
- face_rows: int32 [16, 153], P('domain'), may hold values from 0 to 1223, as said below
Outputs:
- subspace: float32 [19584, 2048], P('domain', 'band')
Inputs may be any that keep to these rules, and one draw needn't show every extreme that they name: `connectivity`: row c lists, for cell c of its slab, the storage rows of the cell's 729 nodes, all different. A value v of 1224 or more names the node held by the upper neighbouring slab in row face_rows[s + 1, v - 1224]. `face_rows`: row s lists the storage rows of slab s's lower face nodes, all different; the storage rows of a slab are a permutation of its 1224 nodes. `cell_matrix`: Symmetric; its diagonal lies between 0.8 and 1.2.
All inputs are finite; a program needn't handle non-finite values.
Results may differ from a plain program's by a relative error of at most 0.0028.
Values may be sent and summed in bfloat16 or wider, within the bound.
A program may use at most 64 MiB of HBM per device.

v0:
```python
import jax
import jax.numpy as jnp
from jax import lax
from jax.sharding import PartitionSpec as P

PANEL = 256
DEGREE = 6


centre = 9.0
half_width = 8.0
highest = lax.Precision.HIGHEST


def from_behind(value, axis, steps):
    count = lax.axis_size(axis)
    leading, last = (max(0, -steps), min(count, count - steps))
    return lax.ppermute(value, axis, [(source, source + steps) for source in range(leading, last)])


def spread(x, axis, root):
    mine = lax.axis_index(axis) == root
    return lax.psum(jnp.where(mine, x, jnp.zeros_like(x)), axis)


def contract(left_side, right_side):
    return jnp.einsum(
        "nk,nj->kj", left_side, right_side, precision=highest, preferred_element_type=jnp.float32
    )


def product(left_side, right_side):
    return jnp.dot(left_side, right_side, precision=highest, preferred_element_type=jnp.float32)


def apply_operator(current, cell_matrix, potential, cell_rows, bottom_rows):
    owned_rows = current.shape[0]
    state_cols = current.shape[1]
    rounded = current.astype(jnp.bfloat16)
    ghosts = from_behind(jnp.take(rounded, bottom_rows, axis=0), "domain", -1)
    extended = jnp.concatenate([rounded, ghosts], axis=0)
    gathered = jnp.take(extended, cell_rows, axis=0)
    local_terms = jnp.einsum(
        "mn,cns->cms", cell_matrix, gathered, preferred_element_type=jnp.float32
    )
    summed = jnp.zeros((extended.shape[0], state_cols), jnp.float32)
    summed = summed.at[cell_rows.reshape(-1)].add(local_terms.reshape(-1, state_cols))
    arrived = from_behind(summed[owned_rows:], "domain", 1)
    summed = summed[:owned_rows].at[bottom_rows].add(arrived)
    return summed + potential[:, None] * current


def chebyshev(states, cell_matrix, potential, cell_rows, bottom_rows):
    previous = states
    current = (
        apply_operator(states, cell_matrix, potential, cell_rows, bottom_rows) - centre * states
    ) / half_width
    for repeat in range(DEGREE - 1):
        following = (
            2.0
            * (
                apply_operator(current, cell_matrix, potential, cell_rows, bottom_rows)
                - centre * current
            )
            / half_width
            - previous
        )
        previous, current = (current, following)
    return current


def panel_columns(states_now, first_root, root_count):
    blocks = [spread(states_now, "band", first_root + number) for number in range(root_count)]
    return jnp.concatenate(blocks, axis=1)


def orthonormalize(panel_cols, targets, weights):
    weighted = panel_cols * weights[:, None]
    gram_matrix = lax.psum(contract(weighted, panel_cols), "domain")
    factor = jnp.linalg.cholesky(gram_matrix)
    basis_cols = jax.scipy.linalg.solve_triangular(factor, panel_cols.T, lower=True).T
    coefficients = lax.psum(contract(basis_cols * weights[:, None], targets), "domain")
    return (basis_cols, coefficients)


def own_slice(basis_cols, offset, state_cols, owners):
    return lax.dynamic_slice_in_dim(
        basis_cols, jnp.clip(offset, 0, owners - 1) * state_cols, state_cols, 1
    )


def per_device(states, potential, node_mass, cell_matrix, connectivity, face_rows):
    band_place = lax.axis_index("band")
    state_cols = states.shape[1]
    owners = PANEL // state_cols
    weights = node_mass / (states.shape[0] * lax.axis_size("domain"))
    bottom_rows = face_rows[0]
    filtered = chebyshev(states, cell_matrix, potential, connectivity, bottom_rows)
    panel_one = panel_columns(filtered, 0, owners)
    basis_one, coefficients = orthonormalize(panel_one, filtered, weights)
    projected = filtered - product(basis_one, coefficients)
    states_now = jnp.where(
        band_place < owners, own_slice(basis_one, band_place, state_cols, owners), projected
    )
    panel_two = panel_columns(states_now, owners, owners)
    basis_two, coefficients = orthonormalize(panel_two, states_now, weights)
    later = states_now - product(basis_two, coefficients)
    second = own_slice(basis_two, band_place - owners, state_cols, owners)
    return jnp.where(
        band_place < owners, states_now, jnp.where(band_place < 2 * owners, second, later)
    )


def solution(mesh):
    return jax.shard_map(
        per_device,
        mesh=mesh,
        in_specs=(
            P("domain", "band"),
            P("domain"),
            P("domain"),
            P(),
            P("domain", None),
            P("domain", None),
        ),
        out_specs=P("domain", "band"),
        check_vma=False,
    )
```

profile of v0, /device:TPU:1, one launch (start us, length us, event | category | flops | bytes accessed | tf_op | source)
XLA Modules:
  0.0 1216.9 jit_solution(8280702898122727736)
XLA Ops:
  11.6 3.8 collective-permute-done
  20.5 9.3 scatter_custom_fusion
  29.8 4.3 collective-permute-start.1
  39.4 3.8 collective-permute-done.2
  48.3 9.3 scatter_custom_fusion.2
  57.6 4.3 collective-permute-start.3
  74.7 4.0 gather_fusion.5
  83.4 10.0 scatter_custom_fusion.4
  94.3 4.2 collective-permute-start.5
  116.0 9.3 scatter_custom_fusion.6
  125.3 3.9 collective-permute-start.7
  148.6 10.0 scatter_custom_fusion.8
  159.5 3.8 collective-permute-start.9
  169.5 3.8 collective-permute-done.10
  178.3 9.3 scatter_custom_fusion.10
  187.7 5.4 collective-permute-start.11
  198.9 170.9 %all-reduce.20.cloned.1.call-done = (f32[1224,128]{1,0:T(8,128)}, f32[1224,128]{1,0:T(8,128)}) async-done(((f32[1224,128]{1,0:T(8,128)}, f32[1224,128]{1,0:T(8,128)}), (f32[1224,128]{1,0:T(8,128)}, f32[1224,128]{1,0:T(8,128)})) %all-reduce.20.cloned.1.call-update) | async-done | bytes 1253392 | tf_op jit(solution)/shard_map/psum | solution.py:23
  374.7 127.1 %all-reduce.10.cloned.1.call-done = f32[256,256]{0,1:T(8,128)} async-done(((f32[256,256]{0,1:T(8,128)}), f32[256,256]{0,1:T(8,128)}) %all-reduce.10.cloned.1.call-update) | async-done | bytes 262160 | tf_op jit(solution)/shard_map/psum | solution.py:79
  503.9 11.7 cholesky.130
  515.7 9.8 custom-call.13
  526.0 11.7 cholesky.147
  539.7 4.0 while.4
  543.7 19.7 %custom-call.14 = f32[2,128,128]{1,2,0:T(8,128)S(1)} custom-call(f32[2,128,128]{2,1,0:T(8,128)S(1)} %get-tuple-element.23), custom_call_target="InvertDiagBlocksLowerTriangular" | custom-call | tf_op jit(solution)/shard_map/jit(_solve_triangular)/triangular_solve | solution.py:81
  570.0 137.4 %all-reduce.12.cloned.1.call-done = f32[256,128]{1,0:T(8,128)} async-done(((f32[256,128]{1,0:T(8,128)}), f32[256,128]{1,0:T(8,128)}) %all-reduce.12.cloned.1.call-update) | async-done | bytes 131088 | tf_op jit(solution)/shard_map/psum | solution.py:82
  710.9 157.6 %all-reduce.18.cloned.1.call-done = (f32[1224,128]{1,0:T(8,128)}, f32[1224,128]{1,0:T(8,128)}) async-done(((f32[1224,128]{1,0:T(8,128)}, f32[1224,128]{1,0:T(8,128)}), (f32[1224,128]{1,0:T(8,128)}, f32[1224,128]{1,0:T(8,128)})) %all-reduce.18.cloned.1.call-update) | async-done | bytes 1253392 | tf_op jit(solution)/shard_map/psum | solution.py:23
  873.2 127.4 %all-reduce.14.cloned.1.call-done = f32[256,256]{0,1:T(8,128)} async-done(((f32[256,256]{0,1:T(8,128)}), f32[256,256]{0,1:T(8,128)}) %all-reduce.14.cloned.1.call-update) | async-done | bytes 262160 | tf_op jit(solution)/shard_map/psum | solution.py:79
  1002.7 11.7 cholesky.164
  1014.5 9.8 custom-call.15
  1024.8 11.7 cholesky.181
  1039.0 4.1 while.5
  1043.1 19.7 %custom-call.16 = f32[2,128,128]{1,2,0:T(8,128)S(1)} custom-call(f32[2,128,128]{2,1,0:T(8,128)S(1)} %get-tuple-element.24), custom_call_target="InvertDiagBlocksLowerTriangular" | custom-call | tf_op jit(solution)/shard_map/jit(_solve_triangular)/triangular_solve | solution.py:81
  1069.4 137.3 %all-reduce.16.cloned.1.call-done = f32[256,128]{1,0:T(8,128)} async-done(((f32[256,128]{1,0:T(8,128)}), f32[256,128]{1,0:T(8,128)}) %all-reduce.16.cloned.1.call-update) | async-done | bytes 131088 | tf_op jit(solution)/shard_map/psum | solution.py:82
  (199 shorter events, 137.1 us)
Async XLA Ops:
  6.5 12.4 %copy-start = (bf16[729,729]{1,0:T(8,128)(2,1)S(1)}, bf16[729,729]{1,0:T(8,128)(2,1)}, u32[]{:S(2)}) copy-start(bf16[729,729]{1,0:T(8,128)(2,1)} %param.16) | copy-start | bytes 3188650
  6.5 4.9 copy-start.19
  6.5 4.8 copy-start.16
  6.5 363.2 %all-reduce.20.cloned.1.call-start = ((), (), s32[]{:S(2)}) async-start(), calls=%async_computation.5 | async-start | bytes 2506752 | tf_op jit(solution)/shard_map/psum | solution.py:23
  10.0 5.4 collective-permute-start
  11.6 9.0 copy-start.17
  19.6 14.5 %copy-start.1 = (f32[1224,128]{1,0:T(8,128)S(1)}, f32[1224,128]{1,0:T(8,128)}, u32[]{:S(2)}) copy-start(f32[1224,128]{1,0:T(8,128)} %param.13) | copy-start | bytes 1880068
  19.6 14.5 %copy-start.15 = (f32[1224]{0:T(1024)S(1)}, f32[1224]{0:T(1024)}, u32[]{:S(2)}) copy-start(f32[1224]{0:T(1024)} %param.14) | copy-start | bytes 14692
  29.8 5.7 collective-permute-start.1
  38.1 5.1 collective-permute-start.2
  57.6 5.7 collective-permute-start.3
  67.8 2.3 copy-start.10
  67.8 30.8 %copy-start.2 = (f32[1224,128]{1,0:T(8,128)}, f32[1224,128]{1,0:T(8,128)S(1)}, u32[]{:S(2)}) copy-start(f32[1224,128]{1,0:T(8,128)S(1)} %get-tuple-element.54) | copy-start | bytes 1880068
  68.6 5.1 collective-permute-start.4
  94.3 6.4 collective-permute-start.5
  106.2 4.7 collective-permute-start.6
  125.3 3.9 copy-start.12
  125.3 6.2 collective-permute-start.7
  129.3 5.4 copy-start.3
  136.8 4.7 collective-permute-start.8
  159.5 5.3 collective-permute-start.9
  168.1 5.1 collective-permute-start.10
  177.4 15.6 %copy-start.7 = (f32[1224,128]{1,0:T(8,128)S(1)}, f32[1224,128]{1,0:T(8,128)}, u32[]{:S(2)}) copy-start(f32[1224,128]{1,0:T(8,128)} %get-tuple-element.48) | copy-start | bytes 1880068
  187.6 5.4 copy-start.11
  187.7 6.8 collective-permute-start.11
  198.8 303.0 %all-reduce.10.cloned.1.call-start = ((), (), s32[]{:S(2)}) async-start(), calls=%async_computation | async-start | bytes 524288 | tf_op jit(solution)/shard_map/psum | solution.py:79
  374.2 333.3 %all-reduce.12.cloned.1.call-start = ((), (), s32[]{:S(2)}) async-start(), calls=%async_computation.1 | async-start | bytes 262144 | tf_op jit(solution)/shard_map/psum | solution.py:82
  566.9 140.6 %copy-start.6 = (f32[1224,128]{1,0:T(8,128)S(1)}, f32[1224,128]{1,0:T(8,128)}, u32[]{:S(2)}) copy-start(f32[1224,128]{1,0:T(8,128)} %copy-done.4) | copy-start | bytes 1880068
  570.0 298.5 %all-reduce.18.cloned.1.call-start = ((), (), s32[]{:S(2)}) async-start(), calls=%async_computation.4 | async-start | bytes 2506752 | tf_op jit(solution)/shard_map/psum | solution.py:23
  710.8 289.8 %all-reduce.14.cloned.1.call-start = ((), (), s32[]{:S(2)}) async-start(), calls=%async_computation.2 | async-start | bytes 524288 | tf_op jit(solution)/shard_map/psum | solution.py:79
  873.0 333.7 %all-reduce.16.cloned.1.call-start = ((), (), s32[]{:S(2)}) async-start(), calls=%async_computation.3 | async-start | bytes 262144 | tf_op jit(solution)/shard_map/psum | solution.py:82
  1066.3 140.4 %copy-start.9 = (f32[1224,128]{1,0:T(8,128)S(1)}, f32[1224,128]{1,0:T(8,128)}, u32[]{:S(2)}) copy-start(f32[1224,128]{1,0:T(8,128)} %get-tuple-element.71) | copy-start | bytes 1880068
  (6 other events, 8.9 us)
Sparse Core Ops, SparseCore 0:
  198.9 170.7 all-reduce.19
  374.3 127.4 all-reduce.9
  570.1 137.3 all-reduce.11
  710.9 157.5 all-reduce.17
  873.1 127.4 all-reduce.13
  1069.5 137.1 all-reduce.15
where the time goes:
time: 1240 us; the launch traced here: 1220 us
  waiting for transfers between devices  881 us (71%)
  other arithmetic  201 us (16%)
  local copies, waits for them, and re-layouts  50 us (4%)
  starting transfers between devices  34.8 us (3%)
  matrix products  32 us (3%)
  between operations  17.3 us (1%)
    psum x2, waiting for transfers between devices, spread(): return lax.psum(jnp.where(mine, x, jnp.zeros_like(x)), axis)  328 us
    psum x2, waiting for transfers between devices, orthonormalize(): lax.psum(contract(basis_cols * weights[:, None], targets), 'domain')  275 us
    psum x2, waiting for transfers between devices, orthonormalize(): gram_matrix = lax.psum(contract(weighted, panel_cols), 'domain')  255 us
    another operation x13, other arithmetic, orthonormalize(): factor = jnp.linalg.cholesky(gram_matrix)  68.5 us
    scatter-add x6, other arithmetic, apply_operator(): summed.at[cell_rows.reshape(-1)].add(local_terms.reshape(-1, state_cols))  57.2 us
    another operation x5, other arithmetic, orthonormalize(): jax.scipy.linalg.solve_triangular(factor, panel_cols.T, lower=True)  39.4 us
    ppermute x12, starting transfers between devices, from_behind(): lax.ppermute(value, axis, [(source, source + steps) for source in range(l...  34 us
  transfers between devices with their start and end apart: 18, of which 16 were waited for; matrix products, arithmetic and copies ran while one was open for 1% of the time, Pallas kernels for 0%

commit v1 on v0

v1 whole, which is shorter than its diff:
```python
import functools
import jax
import jax.numpy as jnp
from jax import lax
from jax.experimental import pallas as pl
from jax.experimental.pallas import tpu as pltpu
from jax.sharding import PartitionSpec as P

f32 = jnp.float32
bf16 = jnp.bfloat16
i32 = jnp.int32
OWNED = 1224
ROWS = 1280
CELL = 729
CP = 768
CS = 1536
FACE = 153
FP = 160
COLS = 128
DEGREE = 6
ND = 16
MESHID = pl.DeviceIdType.MESH
VM = pl.BlockSpec(memory_space=pltpu.VMEM)


def dot(a, b):
    return jnp.dot(a, b, preferred_element_type=f32)


def split2(x):
    hi = x.astype(bf16)
    return hi, (x - hi.astype(f32)).astype(bf16)


def split3(x):
    hi = x.astype(bf16)
    rest = x - hi.astype(f32)
    mid = rest.astype(bf16)
    return hi, mid, (rest - mid.astype(f32)).astype(bf16)


def lanes(shape, base=0):
    return lax.broadcasted_iota(i32, shape, 1) + base


def subs(shape, base=0):
    return lax.broadcasted_iota(i32, shape, 0) + base


def onehot(mask):
    return jnp.where(mask, 1.0, 0.0).astype(bf16)


def filter_kernel(v_ref, pot_ref, mat_ref, conn_ref, face_ref, out_ref,
                  crow, frow, connb, faceb, potb, kp, amat, afac, bmat, gt, ft, gsel, v3, potc, potf, msk,
                  cnt, ws, wb, wf, ybuf, rb, send, recv, vsend, vrecv, ssem, rsem, vsem):
    d = lax.axis_index("domain")
    vrecv[...] = jnp.zeros(vrecv.shape, f32)
    recv[...] = jnp.zeros(recv.shape, f32)
    barrier = pltpu.get_barrier_semaphore()

    for k in (1, ND - 1):
        pl.semaphore_signal(barrier, inc=1, device_id={"domain": lax.rem(d + k, ND)}, device_id_type=MESHID)

    crow[...] = jnp.full(crow.shape, -1.0, f32)
    crow[0:1, 0:CELL] = conn_ref[0:1, :].astype(f32)
    crow[0:1, CP:CP + CELL] = conn_ref[1:2, :].astype(f32)
    frow[...] = jnp.full(frow.shape, -2.0, f32)
    frow[0:1, 0:FACE] = face_ref[0:1, :].astype(f32)
    for t in range(CS // 128):
        row = crow[0:1, 128 * t:128 * t + 128]
        connb[128 * t:128 * t + 128, :] = jnp.broadcast_to(row, (128, 128)).T.astype(i32)
    for t in range(2):
        row = frow[0:1, 128 * t:128 * t + 128]
        faceb[128 * t:128 * t + 128, :] = jnp.broadcast_to(row, (128, 128)).T.astype(i32)
    potb[1152:1280, :] = jnp.zeros((128, 128), f32)
    v3[1216:ROWS, :] = jnp.zeros((ROWS - 1216, 640), bf16)
    for t in range(9):
        row = pot_ref[0:1, 128 * t:128 * t + 128]
        potb[128 * t:128 * t + 128, :] = jnp.broadcast_to(row, (128, 128)).T
    last = jnp.broadcast_to(pot_ref[0:1, OWNED - 128:OWNED], (128, 128)).T
    potb[OWNED - 128:OWNED, :] = last
    hi, mid, lo = split3(v_ref[...])
    v3[0:OWNED, 0:128] = hi
    v3[0:OWNED, 128:256] = mid
    v3[0:OWNED, 256:384] = lo
    hi, lo = split2(potb[0:OWNED, :])
    v3[0:OWNED, 384:512] = hi
    v3[0:OWNED, 512:640] = lo

    fsel = onehot(jnp.tile(faceb[0:FP, :], (1, ROWS // 128)) == lanes((FP, ROWS)))
    fv = dot(fsel, v3[...])
    vface = fv[:, 0:128] + fv[:, 128:256] + fv[:, 256:384]
    potf[...] = fv[:, 384:512] + fv[:, 512:640]
    wf[0] = vface
    wf[1] = jnp.zeros((FP, COLS), f32)
    vsend[...] = vface
    ws[1] = jnp.zeros((CS, COLS), f32)

    pl.semaphore_wait(barrier, 2)

    def vcopy(dst):
        return pltpu.make_async_remote_copy(
            src_ref=vsend, dst_ref=vrecv.at[pl.ds(0, FP), :], send_sem=vsem.at[0], recv_sem=vsem.at[1],
            device_id={"domain": dst}, device_id_type=MESHID)

    @pl.when(d > 0)
    def _():
        vcopy(d - 1).start()

    kp[...] = jnp.zeros(kp.shape, bf16)
    kp[0:CELL, 0:CELL] = mat_ref[...]
    km = kp[...]
    amat[0:CP, 0:CP] = km
    amat[CP:CS, CP:CS] = km
    e01 = onehot(jnp.tile(connb[0:CP, :], (1, CP // 128)) == crow[0:1, CP:CS].astype(i32))
    e01 = jnp.where(jnp.tile(connb[0:CP, :], (1, CP // 128)) >= 0, e01, jnp.zeros_like(e01))
    amat[0:CP, CP:CS] = dot(e01, km).astype(bf16)
    e10 = onehot(jnp.tile(connb[CP:CS, :], (1, CP // 128)) == crow[0:1, 0:CP].astype(i32))
    e10 = jnp.where(jnp.tile(connb[CP:CS, :], (1, CP // 128)) >= 0, e10, jnp.zeros_like(e10))
    amat[CP:CS, 0:CP] = dot(e10, km).astype(bf16)
    ci = crow[0:1, :].astype(i32)
    tup = onehot((subs((FP, CS), OWNED) == ci))
    tlo = onehot(jnp.tile(faceb[0:FP, :], (1, CS // 128)) == ci)
    for c in range(2):
        cols = slice(CP * c, CP * c + CP)
        afac[0:FP, cols] = dot(tup[:, cols], km).astype(bf16)
        afac[FP:2 * FP, cols] = dot(tlo[:, cols], km).astype(bf16)
    fi = frow[0:1, :].astype(i32)
    cb2 = jnp.tile(connb[...], (1, 2))
    bmat[:, 0:256] = onehot(cb2 == fi)
    bmat[:, 256:512] = onehot(cb2 == lanes((CS, 256), OWNED))
    for t in range(ROWS // 128):
        gt[128 * t:128 * t + 128, :] = onehot(subs((128, CS), 128 * t) == ci)
        ft[128 * t:128 * t + 128, :] = onehot(subs((128, 256), 128 * t) == fi)
        gsel[:, 128 * t:128 * t + 128] = onehot(connb[...] == lanes((CS, 128), 128 * t))
    cv = dot(gsel[...], v3[...])
    ws[0] = cv[:, 0:128] + cv[:, 128:256] + cv[:, 256:384]
    potc[...] = cv[:, 384:512] + cv[:, 512:640]
    msk[...] = jnp.where((connb[...] >= OWNED) & (d == ND - 1), 0.0, 1.0)
    cnt[...] = dot(gt[...], jnp.ones((CS, COLS), bf16)) + dot(ft[...], jnp.ones((256, COLS), bf16))

    @pl.when(d < ND - 1)
    def _():
        vcopy(d).wait_recv()

    hi, mid, lo = split3(vrecv[...])
    gv = dot(bmat[:, 256:512], jnp.concatenate([hi, mid, lo], axis=1))
    first = ws[0] + (gv[:, 0:128] + gv[:, 128:256] + gv[:, 256:384])
    ws[0] = first
    wb[...] = first.astype(bf16)

    def up(t, dst):
        return pltpu.make_async_remote_copy(
            src_ref=send.at[t, 0], dst_ref=recv.at[t, pl.ds(0, FP), :], send_sem=ssem.at[t, 0], recv_sem=rsem.at[t, 0],
            device_id={"domain": dst}, device_id_type=MESHID)

    def down(t, dst):
        return pltpu.make_async_remote_copy(
            src_ref=send.at[t, 1], dst_ref=recv.at[t, pl.ds(256, FP), :], send_sem=ssem.at[t, 1], recv_sem=rsem.at[t, 1],
            device_id={"domain": dst}, device_id_type=MESHID)

    def step(t, carry):
        now, then = lax.rem(t, 2), lax.rem(t + 1, 2)
        coef = jnp.where(t == 0, 0.125, 0.25).astype(f32)
        keep = jnp.where(t == 0, 0.0, 1.0).astype(f32)
        x = wb[...]
        fc = dot(afac[...], x)
        wface = wf[now]
        send[t, 0] = fc[0:FP]
        send[t, 1] = fc[FP:2 * FP] + potf[...] * wface

        @pl.when(d < ND - 1)
        def _():
            up(t, d + 1).start()

        @pl.when(d > 0)
        def _():
            down(t, d - 1).start()

        ybuf[...] = dot(amat[...], x)

        @pl.when(d > 0)
        def _():
            up(t, d).wait_recv()
            down(t, d).wait_send()

        @pl.when(d < ND - 1)
        def _():
            down(t, d).wait_recv()
            up(t, d).wait_send()

        got = recv[t]
        wf[then] = coef * (send[t, 1] + got[0:FP] - 9.0 * wface) - keep * wf[then]
        hi, lo = split2(got)
        rb[:, 0:128] = hi
        rb[:, 128:256] = lo
        z = dot(bmat[...], rb[...])
        total = (ybuf[...] + z[:, 0:128] + z[:, 128:256]) * msk[...]
        new = coef * (total + (potc[...] - 9.0) * ws[now]) - keep * ws[then]
        ws[then] = new
        wb[...] = new.astype(bf16)
        return carry

    lax.fori_loop(0, DEGREE, step, 0)

    @pl.when(d > 0)
    def _():
        vcopy(d).wait_send()

    hi, lo = split2(ws[DEGREE % 2])
    back = dot(gt[...], jnp.concatenate([hi, lo], axis=1))
    hi, lo = split2(wf[DEGREE % 2])
    pad = jnp.zeros((256 - FP, 256), bf16)
    fback = dot(ft[...], jnp.concatenate([jnp.concatenate([hi, lo], axis=1), pad], axis=0))
    summed = (back + fback)[0:OWNED]
    count = cnt[0:OWNED, :]
    x = (potb[0:OWNED, :] - 9.0) * 0.125
    x2 = x * x
    alone = ((32.0 * x2 - 48.0) * x2 + 18.0) * x2 - 1.0
    out_ref[...] = jnp.where(count > 0.5, (summed[:, 0:128] + summed[:, 128:256]) / jnp.maximum(count, 1.0), alone * v_ref[...])


def filtered_states(states, potential, cell_matrix, connectivity, face_rows):
    V = pltpu.VMEM
    scratch = [
        V((8, CS), f32), V((8, 256), f32), V((CS, 128), i32), V((256, 128), i32), V((ROWS, 128), f32),
        V((CP, CP), bf16), V((CS, CS), bf16), V((2 * FP, CS), bf16), V((CS, 512), bf16), V((ROWS, CS), bf16),
        V((ROWS, 256), bf16), V((CS, ROWS), bf16), V((ROWS, 640), bf16), V((CS, 128), f32), V((FP, 128), f32),
        V((CS, 128), f32), V((ROWS, 128), f32), V((2, CS, COLS), f32), V((CS, COLS), bf16), V((2, FP, COLS), f32),
        V((CS, COLS), f32), V((512, 256), bf16), V((DEGREE, 2, FP, COLS), f32), V((DEGREE, 512, COLS), f32),
        V((FP, COLS), f32), V((256, COLS), f32),
        pltpu.SemaphoreType.DMA((DEGREE, 2)), pltpu.SemaphoreType.DMA((DEGREE, 2)), pltpu.SemaphoreType.DMA((2,)),
    ]
    return pl.pallas_call(
        filter_kernel,
        out_shape=jax.ShapeDtypeStruct((OWNED, COLS), f32),
        in_specs=[VM] * 5,
        out_specs=VM,
        scratch_shapes=scratch,
        compiler_params=pltpu.CompilerParams(collective_id=0, has_side_effects=True, vmem_limit_bytes=60 << 20),
        name="filter",
    )(states, potential.reshape(1, OWNED), cell_matrix, connectivity, face_rows)
HIGH = lax.Precision.HIGHEST


def nt(a, b, precision=None):
    return lax.dot_general(a, b, (((1,), (1,)), ((), ())), preferred_element_type=f32, precision=precision)


def nn(a, b):
    return jnp.dot(a, b, preferred_element_type=f32, precision=HIGH)


def chol_inverse(block):
    n = 128
    lane = lanes((8, n))
    sub = subs((8, n))
    a = [block[8 * k:8 * k + 8, :] for k in range(n // 8)]
    for j in range(n - 1):
        g, s = j // 8, j % 8
        row = a[g][s:s + 1, :]
        at_j = lane[0:1] == j
        scaled = jnp.where(at_j, 1.0, row) / row[:, j:j + 1]
        for k in range(g, n // 8):
            if k == g and s == 7:
                continue
            col = a[k][:, j:j + 1]
            upd = jnp.where(lane == j, 0.0, a[k]) - col * scaled
            a[k] = jnp.where(sub > s, upd, a[k]) if k == g else upd
    out = []
    for k in range(n // 8):
        here = sub + 8 * k
        diag = jnp.sum(jnp.where(lane == here, a[k], 0.0), axis=1, keepdims=True)
        unit = jnp.where(lane < here, a[k], jnp.where(lane == here, 1.0, 0.0))
        out.append(unit * lax.rsqrt(diag))
    return jnp.concatenate(out, axis=0)


def solve(ext, inv, zbuf, band):
    for i in range(4):
        a, b = 128 * i, 128 * i + 128
        t = chol_inverse(ext[a:b, a:b])
        inv[i] = t
        low = nt(ext[b:640, a:b], t, HIGH)
        ext[b:640, a:b] = low
        if i < 3:
            ext[b:640, b:512] = ext[b:640, b:512] - nt(low, low[0:512 - b], HIGH)
    eye = jnp.where(lanes((128, 128)) == subs((128, 128)), 1.0, 0.0)
    for i in (3, 2, 1, 0):
        a, b = 128 * i, 128 * i + 128
        y = jnp.where(band < 4, jnp.where(band == i, -eye, 0.0), ext[512:640, a:b])
        if i < 3:
            y = y - nn(zbuf[:, b:512], ext[b:512, a:b])
        zbuf[:, a:b] = nn(y, inv[i])


def peer(axis, index):
    return {axis: index}


def ortho(own_ref, mass_ref, out_ref, d, band, wgt, pan, wt, sbuf, rsbuf, agbuf, gbuf, ext, inv, zbuf, wcol,
          asem_s, asem_r, bsem_s, bsem_r, csem_s, csem_r, dsem_s, dsem_r, fsem_s,
          rs_s, rs_r, gg_s, gg_r, gm_s, gm_r, gx_s, gx_r, gy_s, gy_r):
    x = band // 4
    yh = lax.rem(band // 2, 2)
    c = lax.rem(band, 2)
    mine = lax.rem(band, 4)
    half = ROWS // 2

    def copy(src, dst, ss, rs, to):
        return pltpu.make_async_remote_copy(src_ref=src, dst_ref=dst, send_sem=ss, recv_sem=rs,
                                            device_id={"band": to}, device_id_type=MESHID)

    def part(block, h):
        return pan.at[block, pl.ds(h * half, half), :]

    def acopy(h, slot, to):
        return copy(part(mine, h), part(mine, h), asem_s.at[slot, h], asem_r.at[h], to)

    y_peer = x * 4 + (1 - yh) * 2 + c
    c_peer = x * 4 + yh * 2 + (1 - c)
    across = (1 - yh) * 2 + c
    own = own_ref[0:OWNED, :]

    @pl.when(x == 0)
    def _():
        pan[mine, 0:OWNED, :] = own.astype(bf16)
        pan[mine, OWNED:ROWS, :] = jnp.zeros((ROWS - OWNED, COLS), bf16)
        acopy(0, 0, band + 4).start()
        acopy(1, 1, band + 12).start()
        acopy(1, 0, band + 4).start()
        acopy(0, 1, band + 12).start()

    first = jnp.where(x == 3, 1, 0)

    def bcopy(h):
        return copy(part(mine, h), part(mine, h), bsem_s.at[h], bsem_r.at[h], y_peer)

    def ccopy(h):
        return copy(part(mine, h), part(mine, h), csem_s.at[h], csem_r.at[h], c_peer)

    def dcopy(h):
        return copy(part(across, h), part(across, h), dsem_s.at[h], dsem_r.at[h], c_peer)

    for k in range(2):
        h = lax.rem(first + k, 2)

        @pl.when(x > 0)
        def _():
            acopy(h, 0, band).wait_recv()

        if k == 0:
            @pl.when((x == 1) | (x == 3))
            def _():
                copy(part(mine, h), part(mine, h), fsem_s.at[0], asem_r.at[h], lax.rem(band, 4) + 8).start()
        bcopy(h).start()
        ccopy(h).start()

    for t in range(10):
        lo_row, hi_row = 128 * t, min(128 * t + 128, OWNED)
        if hi_row - lo_row == 128:
            row = mass_ref[0:1, lo_row:hi_row]
            wgt[lo_row:hi_row, :] = jnp.broadcast_to(row, (128, 128)).T * (1.0 / (ND * OWNED))
        else:
            wgt[lo_row:ROWS, :] = jnp.zeros((ROWS - lo_row, 128), f32)
            row = mass_ref[0:1, OWNED - 128:OWNED]
            wgt[OWNED - 128:OWNED, :] = jnp.broadcast_to(row, (128, 128)).T * (1.0 / (ND * OWNED))
    wcol[0:OWNED, :] = own * wgt[0:OWNED, :]
    wcol[OWNED:ROWS, :] = jnp.zeros((ROWS - OWNED, COLS), f32)
    for t in range(10):
        hi, lo = split2(wcol[128 * t:128 * t + 128, :].T)
        wt[0:128, 128 * t:128 * t + 128] = hi
        wt[128:256, 128 * t:128 * t + 128] = lo

    for k in range(2):
        h = lax.rem(first + k, 2)
        copy(part(across, h), part(across, h), bsem_s.at[h], bsem_r.at[h], y_peer).wait_recv()
        dcopy(h).start()
    for h in range(2):
        copy(part(mine, h), part(mine, h), csem_s.at[h], csem_r.at[h], c_peer).wait_recv()
        copy(part(mine, h), part(mine, h), dsem_s.at[h], dsem_r.at[h], c_peer).wait_recv()

    wcol[...] = pan[x].astype(f32) * wgt[...]
    pair = [jnp.concatenate([pan[0], pan[1]], axis=1), jnp.concatenate([pan[2], pan[3]], axis=1)]
    for t in range(10):
        ext[0:128, 0:128] = wcol[128 * t:128 * t + 128, :].T
        hi, lo = split2(ext[pl.ds(pl.multiple_of(lax.rem(band, 4) * 32, 32), 32), 0:128])
        wt[256:288, 128 * t:128 * t + 128] = hi
        wt[288:320, 128 * t:128 * t + 128] = lo
    for q in range(2):
        r = dot(wt[...], pair[q])
        sbuf[:, 256 * q:256 * q + 256] = r[0:128] + r[128:256]
        ext[0:32, 256 * q:256 * q + 256] = r[256:288] + r[288:320]
    for m in range(ND):
        sbuf[8 * m:8 * m + 8, 512:640] = ext[8 * (m // 4):8 * (m // 4) + 8, 128 * (m % 4):128 * (m % 4) + 128]

    def rows(m):
        return pl.ds(pl.multiple_of(m * 8, 8), 8)

    def rs(src_rows, slot, ss, to):
        return pltpu.make_async_remote_copy(
            src_ref=sbuf.at[rows(src_rows), :], dst_ref=rsbuf.at[slot], send_sem=rs_s.at[ss], recv_sem=rs_r.at[slot],
            device_id={"domain": to}, device_id_type=MESHID)

    for k in range(1, ND):
        to = lax.rem(d + k, ND)
        rs(to, d, k, to).start()
    rsbuf[d] = sbuf[rows(d), :]
    for k in range(1, ND):
        frm = lax.rem(d + k, ND)
        rs(frm, frm, k, frm).wait_recv()
    total = rsbuf[0]
    for m in range(1, ND):
        total = total + rsbuf[m]
    agbuf[rows(d), :] = total

    def ag(col, width, who, ss, rr, k, to):
        view = agbuf.at[rows(who), pl.ds(col, width)]
        return pltpu.make_async_remote_copy(
            src_ref=view, dst_ref=view, send_sem=ss.at[k], recv_sem=rr.at[who],
            device_id={"domain": to}, device_id_type=MESHID)

    for k in range(1, ND):
        to = lax.rem(d + k, ND)
        ag(512, 128, d, gg_s, gg_r, k, to).start()
    for k in range(1, ND):
        to = lax.rem(d + k, ND)
        ag(0, 512, d, gm_s, gm_r, k, to).start()
    for k in range(1, ND):
        frm = lax.rem(d + k, ND)
        ag(512, 128, frm, gg_s, gg_r, k, frm).wait_recv()

    gbuf[band] = agbuf[:, 512:640]
    chip = band // 2

    def strip(who, ss, rr, k, to):
        return copy(gbuf.at[who], gbuf.at[who], ss.at[k], rr.at[who], to)

    for k in range(1, 8):
        to = lax.rem(chip + k, 8) * 2 + c
        strip(band, gx_s, gx_r, k, to).start()
    strip(band, gy_s, gy_r, 0, c_peer).start()
    for k in range(1, 8):
        frm = lax.rem(chip + k, 8) * 2 + c
        strip(frm, gx_s, gx_r, k, frm).wait_recv()
        strip(frm, gy_s, gy_r, k, c_peer).start()
    for k in range(8):
        frm = lax.rem(chip + k, 8) * 2 + (1 - c)
        strip(frm, gy_s, gy_r, k, c_peer).wait_recv()

    for b in range(16):
        for m in range(ND):
            ext[32 * b + 8 * (m // 4):32 * b + 8 * (m // 4) + 8, 128 * (m % 4):128 * (m % 4) + 128] = gbuf[b, 8 * m:8 * m + 8, :]
    for k in range(1, ND):
        frm = lax.rem(d + k, ND)
        ag(0, 512, frm, gm_s, gm_r, k, frm).wait_recv()
    ext[512:640, :] = agbuf[:, 0:512]

    solve(ext, inv, zbuf, band)

    zh, zl = split2(zbuf[...])
    zz = jnp.concatenate([zh, zl], axis=0)
    prod = nt(pair[0], zz[:, 0:256]) + nt(pair[1], zz[:, 256:512])
    update = prod[0:OWNED, 0:128] + prod[0:OWNED, 128:256]
    is_panel = band < 4
    zown = zbuf[:, pl.ds(pl.multiple_of(jnp.minimum(band, 3) * 128, 128), 128)]
    rest = (own - own.astype(bf16).astype(f32)).astype(bf16)
    fix = nt(rest, zown.astype(bf16))
    out_ref[...] = jnp.where(is_panel, -update - fix, own - update)

    @pl.when(x == 0)
    def _():
        for h in range(2):
            acopy(h, 0, band).wait_send()
            acopy(h, 1, band).wait_send()

    @pl.when((x == 1) | (x == 3))
    def _():
        copy(part(mine, 0), part(mine, 0), fsem_s.at[0], asem_r.at[0], band).wait_send()

    for h in range(2):
        bcopy(h).wait_send()
        ccopy(h).wait_send()
        dcopy(h).wait_send()
    for k in range(1, ND):
        rs(d, d, k, d).wait_send()
        ag(512, 128, d, gg_s, gg_r, k, d).wait_send()
        ag(0, 512, d, gm_s, gm_r, k, d).wait_send()
    for k in range(1, 8):
        strip(band, gx_s, gx_r, k, band).wait_send()
    for k in range(8):
        strip(band, gy_s, gy_r, k, band).wait_send()


def ortho_kernel(own_ref, mass_ref, out_ref, *scratch):
    d = lax.axis_index("domain")
    band = lax.axis_index("band")
    barrier = pltpu.get_barrier_semaphore()
    for k in range(1, 16):
        pl.semaphore_signal(barrier, inc=1, device_id={"domain": lax.rem(d + k, ND)}, device_id_type=MESHID)
        pl.semaphore_signal(barrier, inc=1, device_id={"band": lax.rem(band + k, 16)}, device_id_type=MESHID)
    pl.semaphore_wait(barrier, 30)
    ortho(own_ref, mass_ref, out_ref, d, band, *scratch)


def orthonormal_states(own, mass):
    V = pltpu.VMEM
    D = pltpu.SemaphoreType.DMA
    scratch = [
        V((ROWS, 128), f32), V((4, ROWS, COLS), bf16), V((320, ROWS), bf16), V((128, 640), f32), V((ND, 8, 640), f32),
        V((128, 640), f32), V((16, 128, 128), f32), V((640, 512), f32), V((4, 128, 128), f32), V((128, 512), f32),
        V((ROWS, COLS), f32),
        D((2, 2)), D((2,)), D((2,)), D((2,)), D((2,)), D((2,)), D((2,)), D((2,)), D((1,)),
        D((ND,)), D((ND,)), D((ND,)), D((ND,)), D((ND,)), D((ND,)), D((8,)), D((16,)), D((8,)), D((16,)),
    ]
    return pl.pallas_call(
        ortho_kernel,
        out_shape=jax.ShapeDtypeStruct((OWNED, COLS), f32),
        in_specs=[VM] * 2,
        out_specs=VM,
        scratch_shapes=scratch,
        compiler_params=pltpu.CompilerParams(collective_id=1, has_side_effects=True, vmem_limit_bytes=60 << 20),
        name="orthonormalize",
    )(own, mass.reshape(1, OWNED))


def per_device(states, potential, node_mass, cell_matrix, connectivity, face_rows):
    filtered = filtered_states(states, potential, cell_matrix, connectivity, face_rows)
    return orthonormal_states(filtered, node_mass)


def solution(mesh):
    return jax.shard_map(
        per_device, mesh=mesh,
        in_specs=(P("domain", "band"), P("domain"), P("domain"), P(), P("domain", None), P("domain", None)),
        out_specs=P("domain", "band"), check_vma=False,
    )
```

time: 1240 us -> 166 us (0.13); the launches traced: 1220 us -> 166 us
  waiting for transfers between devices: 881 us -> 0 us
  other arithmetic: 201 us -> 0 us
  Pallas kernels: 0 us -> 161 us
  local copies, waits for them, and re-layouts: 50 us -> 4.53 us
  starting transfers between devices: 34.8 us -> 0 us
  matrix products: 32 us -> 0 us
  between operations: 17.3 us -> 0.02 us
    psum x6 -> x0, waiting for transfers between devices: 858 us -> none  [the longest x2 328 us: spread(): return lax.psum(jnp.where(mine, x, jnp.zeros_like(x)), axis)]
    pallas_call x0 -> x2, Pallas kernels: none -> 161 us  [the longest x1 113 us: orthonormal_states(): pl.pallas_call(ortho_kernel, out_shape=jax.ShapeDtypeStruct((OWNED, COLS)...]
    another operation x24 -> x0, other arithmetic: 116 us -> none  [the longest x13 68.5 us: orthonormalize(): factor = jnp.linalg.cholesky(gram_matrix)]
    scatter-add x12 -> x0, other arithmetic: 71.4 us -> none  [the longest x6 57.2 us: apply_operator(): summed.at[cell_rows.reshape(-1)].add(local_terms.reshape(-1, state_cols))]
    ppermute x12 -> x0, starting transfers between devices: 34 us -> none  [from_behind(): lax.ppermute(value, axis, [(source, source + steps) for source in range(l...]
    gather x18 -> x0, local copies, waits for them, and re-layouts: 26.9 us -> none  [the longest x12 22.4 us: apply_operator(): gathered = jnp.take(extended, cell_rows, axis=0)]
    dot_general x12 -> x0, matrix products: 24.2 us -> none  [the longest x4 12.4 us: contract(): jnp.einsum('nk,nj->kj', left_side, right_side, precision=highest, preferr...]
    ppermute x12 -> x0, waiting for transfers between devices: 23.6 us -> none  [from_behind(): lax.ppermute(value, axis, [(source, source + steps) for source in range(l...]
  transfers between devices with their start and end apart: 18 -> 0, of which waited for: 16 -> 0; matrix products, arithmetic and copies ran while one was open for 1% -> 0% of each run, Pallas kernels for 0% -> 0%
where the time goes in v1:
time: 166 us
  Pallas kernels  161 us (97%)
  local copies, waits for them, and re-layouts  4.53 us (3%)
    pallas_call x1, Pallas kernels, orthonormal_states(): pl.pallas_call(ortho_kernel, out_shape=jax.ShapeDtypeStruct((OWNED, COLS)...  113 us
    pallas_call x1, Pallas kernels, filtered_states(): pl.pallas_call(filter_kernel, out_shape=jax.ShapeDtypeStruct((OWNED, COLS...  47.8 us

profile of v1, /device:TPU:1, one launch (start us, length us, event | category | flops | bytes accessed | tf_op | source)
XLA Modules:
  0.0 165.6 jit_solution(6727760986450202050)
XLA Ops:
  0.0 1.3 reshape.6.pot_ref
  1.3 1.3 reshape.7.mass_ref
  2.6 47.8 %filter.1.own_ref = f32[1224,128]{1,0:T(8,128)} custom-call(f32[1224,128]{1,0:T(8,128)} %v_ref.1, f32[1,1224]{1,0:T(1,128)} %reshape.6.pot_ref, bf16[729,729]{1,0:T(8,128)(2,1)} %mat_ref.1, s32[2,729]{1,0:T(2,128)} %conn_ref.1, s32[1,153]{1,0:T(1,128)} %face_ref.1), custom_call_target="tpu_custom_call" | custom-call | tf_op jit(solution)/shard_map/filter/pallas_call | solution.py:235
  50.4 113.3 %orthonormalize.1 = f32[1224,128]{1,0:T(8,128)} custom-call(f32[1224,128]{1,0:T(8,128)} %filter.1.own_ref, f32[1,1224]{1,0:T(1,128)} %reshape.7.mass_ref), custom_call_target="tpu_custom_call" | custom-call | tf_op jit(solution)/shard_map/orthonormalize/pallas_call | solution.py:517
  163.7 1.9 %copy.8 = f32[1224,128]{1,0:T(8,128)} copy(f32[1224,128]{1,0:T(8,128)} %orthonormalize.1) | data formatting | bytes 1253376

commit v2 on v1

v2 whole, which is shorter than its diff:
```python
import functools
import jax
import jax.numpy as jnp
from jax import lax
from jax.experimental import pallas as pl
from jax.experimental.pallas import tpu as pltpu
from jax.sharding import PartitionSpec as P

f32 = jnp.float32
bf16 = jnp.bfloat16
i32 = jnp.int32
OWNED = 1224
ROWS = 1280
CELL = 729
CP = 768
CS = 1536
FACE = 153
FP = 160
COLS = 128
DEGREE = 6
ND = 16
MESHID = pl.DeviceIdType.MESH
VM = pl.BlockSpec(memory_space=pltpu.VMEM)


def dot(a, b):
    return jnp.dot(a, b, preferred_element_type=f32)


def split2(x):
    hi = x.astype(bf16)
    return hi, (x - hi.astype(f32)).astype(bf16)


def split3(x):
    hi = x.astype(bf16)
    rest = x - hi.astype(f32)
    mid = rest.astype(bf16)
    return hi, mid, (rest - mid.astype(f32)).astype(bf16)


def lanes(shape, base=0):
    return lax.broadcasted_iota(i32, shape, 1) + base


def subs(shape, base=0):
    return lax.broadcasted_iota(i32, shape, 0) + base


def onehot(mask):
    return jnp.where(mask, 1.0, 0.0).astype(bf16)


HIGH = lax.Precision.HIGHEST


def nt(a, b, precision=None):
    return lax.dot_general(a, b, (((1,), (1,)), ((), ())), preferred_element_type=f32, precision=precision)


def nn(a, b):
    return jnp.dot(a, b, preferred_element_type=f32, precision=HIGH)


def chol_inverse(block):
    n = 128
    shape = (8, n)
    lane = lanes(shape)
    sub = subs(shape)
    a = [block[8 * k:8 * k + 8, :] for k in range(n // 8)]
    out = []
    for g in range(n // 8):
        j0 = 8 * g
        inside = (lane >= j0) & (lane < j0 + 8)
        here = a[g]
        cols = [jnp.broadcast_to(here[:, j0 + k:j0 + k + 1], shape) for k in range(8)]
        s = {(i, k): jnp.broadcast_to(cols[k][i:i + 1, :], shape) for k in range(8) for i in range(k, 8)}
        r = [jnp.where(inside, 0.0, jnp.broadcast_to(here[i:i + 1, :], shape)) for i in range(8)]
        inv, done = [], None
        for k in range(8):
            root = lax.rsqrt(s[k, k])
            inv.append(root * root)
            r[k] = jnp.where(lane == j0 + k, 1.0, r[k])
            for i in range(k + 1, 8):
                m = s[i, k] * inv[k]
                for q in range(k + 1, i + 1):
                    s[i, q] = s[i, q] - m * s[q, k]
                r[i] = r[i] - m * r[k]
            row = r[k] * root
            done = row if done is None else jnp.where(sub == k, row, done)
        out.append(jnp.where(lane <= sub + j0, done, 0.0))
        for t in range(g + 1, n // 8):
            c = [jnp.broadcast_to(a[t][:, j0 + k:j0 + k + 1], shape) for k in range(8)]
            acc = jnp.where(inside, 0.0, a[t])
            for k in range(8):
                m = c[k] * inv[k]
                for q in range(k + 1, 8):
                    c[q] = c[q] - m * s[q, k]
                acc = acc - m * r[k]
            a[t] = acc
    return jnp.concatenate(out, axis=0)


def factor(ext, inv):
    for i in range(4):
        a, b = 128 * i, 128 * i + 128
        t = chol_inverse(ext[a:b, a:b])
        inv[i] = t
        if i < 3:
            low = nt(ext[b:512, a:b], t, HIGH)
            ext[b:512, a:b] = low
            ext[b:512, b:512] = ext[b:512, b:512] - nt(low, low, HIGH)


def solve(ext, inv, m_ref, ybuf, zbuf, band):
    for i in range(4):
        a, b = 128 * i, 128 * i + 128
        y = m_ref[:, a:b]
        if i > 0:
            y = y - nt(ybuf[:, 0:a], ext[a:b, 0:a], HIGH)
        ybuf[:, a:b] = nt(y, inv[i], HIGH)
    eye = jnp.where(lanes((128, 128)) == subs((128, 128)), 1.0, 0.0)
    for i in (3, 2, 1, 0):
        a, b = 128 * i, 128 * i + 128
        y = jnp.where(band < 4, jnp.where(band == i, -eye, 0.0), ybuf[:, a:b])
        if i < 3:
            y = y - nn(zbuf[:, b:512], ext[b:512, a:b])
        zbuf[:, a:b] = nn(y, inv[i])


NCH = 6
CH = 208


def filter_states(d, barrier_wait, v_ref, pot_ref, mass_ref, mat_ref, conn_ref, face_ref, own,
                  crow, frow, connb, faceb, potb, kp, amat, afac, bmat, gt, ft, gsel, v3, potc, potf, msk,
                  cnt, ws, wb, wf, ybuf, send, recv, vsend, vrecv, ssem, rsem, vsem, wgt):
    crow[...] = jnp.full(crow.shape, -1.0, f32)
    crow[0:1, 0:CELL] = conn_ref[0:1, :].astype(f32)
    crow[0:1, CP:CP + CELL] = conn_ref[1:2, :].astype(f32)
    frow[...] = jnp.full(frow.shape, -2.0, f32)
    frow[0:1, 0:FACE] = face_ref[0:1, :].astype(f32)
    for t in range(2):
        row = frow[0:1, 128 * t:128 * t + 128]
        faceb[128 * t:128 * t + 128, :] = jnp.broadcast_to(row, (128, 128)).T.astype(i32)
    potb[1152:1280, :] = jnp.zeros((128, 128), f32)
    v3[1216:ROWS, :] = jnp.zeros((ROWS - 1216, 512), bf16)
    for t in range(9):
        row = pot_ref[0:1, 128 * t:128 * t + 128]
        potb[128 * t:128 * t + 128, :] = jnp.broadcast_to(row, (128, 128)).T
    potb[OWNED - 128:OWNED, :] = jnp.broadcast_to(pot_ref[0:1, OWNED - 128:OWNED], (128, 128)).T
    hi, lo = split2(v_ref[...])
    v3[0:OWNED, 0:128] = hi
    v3[0:OWNED, 128:256] = lo
    hi, lo = split2(potb[0:OWNED, :])
    v3[0:OWNED, 256:384] = hi
    v3[0:OWNED, 384:512] = lo

    fsel = onehot(jnp.tile(faceb[0:FP, :], (1, ROWS // 128)) == lanes((FP, ROWS)))
    fv = dot(fsel, v3[...])
    vface = fv[:, 0:128] + fv[:, 128:256]
    potf[...] = fv[:, 256:384] + fv[:, 384:512]
    wf[0] = vface
    wf[1] = jnp.zeros((FP, COLS), f32)
    vsend[...] = vface.astype(bf16)
    ws[1] = jnp.zeros((CS, COLS), f32)
    barrier_wait()

    def vcopy(dst):
        return pltpu.make_async_remote_copy(
            src_ref=vsend, dst_ref=vrecv.at[pl.ds(0, FP), :], send_sem=vsem.at[0], recv_sem=vsem.at[1],
            device_id={"domain": dst}, device_id_type=MESHID)

    @pl.when(d > 0)
    def _():
        vcopy(d - 1).start()

    for t in range(CS // 128):
        row = crow[0:1, 128 * t:128 * t + 128]
        connb[128 * t:128 * t + 128, :] = jnp.broadcast_to(row, (128, 128)).T.astype(i32)
    kp[...] = jnp.zeros(kp.shape, bf16)
    kp[0:CELL, 0:CELL] = mat_ref[...]
    ci = crow[0:1, :].astype(i32)
    fi = frow[0:1, :].astype(i32)
    tup = onehot(subs((FP, CS), OWNED) == ci)
    tlo = onehot(jnp.tile(faceb[0:FP, :], (1, CS // 128)) == ci)
    both = jnp.concatenate([tup, tlo], axis=0)
    for c in range(2):
        cols = slice(CP * c, CP * c + CP)
        afac[:, cols] = dot(both[:, cols], kp[...]).astype(bf16)
    for t in range(ROWS // 128):
        gsel[:, 128 * t:128 * t + 128] = onehot(connb[...] == lanes((CS, 128), 128 * t))
    cv = dot(gsel[...], v3[...])
    ws[0] = cv[:, 0:128] + cv[:, 128:256]
    potc[...] = cv[:, 256:384] + cv[:, 384:512]
    cb2 = jnp.tile(connb[...], (1, 2))
    bmat[:, 0:256] = onehot(cb2 == fi)
    bmat[:, 256:512] = onehot(cb2 == lanes((CS, 256), OWNED))
    msk[...] = jnp.where((connb[...] >= OWNED) & (d == ND - 1), 0.0, 1.0)

    @pl.when(d < ND - 1)
    def _():
        vcopy(d).wait_recv()

    first = ws[0] + dot(bmat[:, 256:512], vrecv[...])
    ws[0] = first
    wb[...] = first.astype(bf16)

    def up(t, dst):
        return pltpu.make_async_remote_copy(
            src_ref=send.at[t, 0], dst_ref=recv.at[t, pl.ds(0, FP), :], send_sem=ssem.at[t, 0], recv_sem=rsem.at[t, 0],
            device_id={"domain": dst}, device_id_type=MESHID)

    def down(t, dst):
        return pltpu.make_async_remote_copy(
            src_ref=send.at[t, 1], dst_ref=recv.at[t, pl.ds(256, FP), :], send_sem=ssem.at[t, 1], recv_sem=rsem.at[t, 1],
            device_id={"domain": dst}, device_id_type=MESHID)

    def step(t, carry):
        now, then = lax.rem(t, 2), lax.rem(t + 1, 2)
        coef = jnp.where(t == 0, 0.125, 0.25).astype(f32)
        keep = jnp.where(t == 0, 0.0, 1.0).astype(f32)
        x = wb[...]
        fc = dot(afac[...], x)
        wface = wf[now]
        lower = fc[FP:2 * FP] + potf[...] * wface
        send[t, 0] = fc[0:FP].astype(bf16)
        send[t, 1] = lower.astype(bf16)

        @pl.when(d < ND - 1)
        def _():
            up(t, d + 1).start()

        @pl.when(d > 0)
        def _():
            down(t, d - 1).start()

        @pl.when(t == 0)
        def _():
            km = kp[...]
            amat[0:CP, 0:CP] = km
            amat[CP:CS, CP:CS] = km
            none = jnp.zeros((CP, CP), bf16)
            c0 = jnp.tile(connb[0:CP, :], (1, CP // 128))
            e01 = jnp.where(c0 >= 0, onehot(c0 == crow[0:1, CP:CS].astype(i32)), none)
            amat[0:CP, CP:CS] = dot(e01, km).astype(bf16)
            c1 = jnp.tile(connb[CP:CS, :], (1, CP // 128))
            e10 = jnp.where(c1 >= 0, onehot(c1 == crow[0:1, 0:CP].astype(i32)), none)
            amat[CP:CS, 0:CP] = dot(e10, km).astype(bf16)

        ybuf[...] = dot(amat[...], x)

        @pl.when(t < 5)
        def _():
            at = pl.ds(pl.multiple_of(256 * t, 256), 256)
            g = onehot(subs((256, CS), 256 * t) == ci)
            h = onehot(subs((256, 256), 256 * t) == fi)
            gt[at, :] = g
            ft[at, :] = h
            cnt[at, :] = dot(g, jnp.ones((CS, COLS), bf16)) + dot(h, jnp.ones((256, COLS), bf16))

        @pl.when(t == 5)
        def _():
            for s in range(9):
                row = mass_ref[0:1, 128 * s:128 * s + 128]
                wgt[128 * s:128 * s + 128, :] = jnp.broadcast_to(row, (128, 128)).T * (1.0 / (ND * OWNED))
            wgt[1152:ROWS, :] = jnp.zeros((ROWS - 1152, 128), f32)
            row = mass_ref[0:1, OWNED - 128:OWNED]
            wgt[OWNED - 128:OWNED, :] = jnp.broadcast_to(row, (128, 128)).T * (1.0 / (ND * OWNED))

        @pl.when(d > 0)
        def _():
            up(t, d).wait_recv()
            down(t, d).wait_send()

        @pl.when(d < ND - 1)
        def _():
            down(t, d).wait_recv()
            up(t, d).wait_send()

        got = recv[t]
        wf[then] = coef * (lower + got[0:FP].astype(f32) - 9.0 * wface) - keep * wf[then]
        total = (ybuf[...] + dot(bmat[...], got)) * msk[...]
        new = coef * (total + (potc[...] - 9.0) * ws[now]) - keep * ws[then]
        ws[then] = new
        wb[...] = new.astype(bf16)
        return carry

    lax.fori_loop(0, DEGREE, step, 0)

    @pl.when(d > 0)
    def _():
        vcopy(d).wait_send()

    hi, lo = split2(ws[DEGREE % 2])
    back = dot(gt[...], jnp.concatenate([hi, lo], axis=1))
    hi, lo = split2(wf[DEGREE % 2])
    pad = jnp.zeros((256 - FP, 256), bf16)
    fback = dot(ft[...], jnp.concatenate([jnp.concatenate([hi, lo], axis=1), pad], axis=0))
    summed = (back + fback)[0:OWNED]
    count = cnt[0:OWNED, :]
    x = (potb[0:OWNED, :] - 9.0) * 0.125
    x2 = x * x
    alone = ((32.0 * x2 - 48.0) * x2 + 18.0) * x2 - 1.0
    own[0:OWNED, :] = jnp.where(count > 0.5, (summed[:, 0:128] + summed[:, 128:256]) / jnp.maximum(count, 1.0), alone * v_ref[...])
    own[OWNED:ROWS, :] = jnp.zeros((ROWS - OWNED, COLS), f32)


def strip_of(band):
    x = band // 4
    return 4 * (2 * lax.rem(band // 2, 2) + x // 2) + lax.rem(x, 2) * 2 + lax.rem(band, 2)


def ortho(own_ref, out_ref, d, band, wgt, pan, wt, sbm, rsm, sbg, rsg, agg, agm, gbuf, stripbuf, ext, inv, ybuf, zbuf, wcol,
          asem_s, asem_r, bsem_s, bsem_r, csem_s, csem_r, dsem_s, dsem_r, fsem_s,
          rg_s, rg_r, rm_s, rm_r, gg_s, gg_r, gm_s, gm_r, gx_s, gx_r, gy_s, gy_r):
    x = band // 4
    yh = lax.rem(band // 2, 2)
    c = lax.rem(band, 2)
    mine = lax.rem(band, 4)

    def copy(src, dst, ss, rs, to):
        return pltpu.make_async_remote_copy(src_ref=src, dst_ref=dst, send_sem=ss, recv_sem=rs,
                                            device_id={"band": to}, device_id_type=MESHID)

    def part(block, h):
        return pan.at[block, pl.ds(pl.multiple_of(h * CH, 16), CH), :]

    def acopy(h, slot, to):
        return copy(part(mine, h), part(mine, h), asem_s.at[slot, h], asem_r.at[h], to)

    y_peer = x * 4 + (1 - yh) * 2 + c
    c_peer = x * 4 + yh * 2 + (1 - c)
    across = (1 - yh) * 2 + c

    @pl.when(x == 0)
    def _():
        pan[mine, 0:NCH * CH, :] = own_ref[0:NCH * CH, :].astype(bf16)
        for k in range(NCH):
            acopy(k, 0, band + 4).start()
            acopy((k + 3) % NCH, 1, band + 12).start()

    def order(k):
        return jnp.where(x == 3, (k + 3) % NCH, jnp.where(x == 2, (k % 2) * 3 + k // 2, k))

    def bcopy(h):
        return copy(part(mine, h), part(mine, h), bsem_s.at[h], bsem_r.at[h], y_peer)

    def ccopy(h):
        return copy(part(mine, h), part(mine, h), csem_s.at[h], csem_r.at[h], c_peer)

    def dcopy(h):
        return copy(part(across, h), part(across, h), dsem_s.at[h], dsem_r.at[h], c_peer)

    def fcopy(h, k, to):
        return copy(part(mine, h), part(mine, h), fsem_s.at[k], asem_r.at[h], to)

    for k in range(NCH):
        h = order(k)

        @pl.when(x > 0)
        def _():
            acopy(h, 0, band).wait_recv()

        if k < 3:
            @pl.when((x == 1) | (x == 3))
            def _():
                fcopy(h, k, mine + 8).start()
        bcopy(h).start()
        ccopy(h).start()

    for t in range(10):
        at = slice(128 * t, 128 * t + 128)
        hi, lo = split2((own_ref[at, :] * wgt[at, :]).T)
        wt[0:128, at] = hi
        wt[128:256, at] = lo

    for h in range(NCH):
        copy(part(mine, h), part(mine, h), csem_s.at[h], csem_r.at[h], c_peer).wait_recv()
    wcol[...] = pan[2 * yh + x // 2].astype(f32) * wgt[...]
    sub = pl.multiple_of((lax.rem(x, 2) * 2 + c) * 32, 32)
    for t in range(10):
        at = slice(128 * t, 128 * t + 128)
        ybuf[0:128, 0:128] = wcol[at, :].T
        hi, lo = split2(ybuf[pl.ds(sub, 32), 0:128])
        wt[256:288, at] = hi
        wt[288:320, at] = lo

    def rows(m):
        return pl.ds(pl.multiple_of(m * 8, 8), 8)

    def rm(p, src_rows, slot, ss, to):
        return pltpu.make_async_remote_copy(
            src_ref=sbm.at[p, rows(src_rows), :], dst_ref=rsm.at[p, slot], send_sem=rm_s.at[p, ss], recv_sem=rm_r.at[p, slot],
            device_id={"domain": to}, device_id_type=MESHID)

    def rg(src_rows, slot, ss, to):
        return pltpu.make_async_remote_copy(
            src_ref=sbg.at[rows(src_rows), :], dst_ref=rsg.at[slot], send_sem=rg_s.at[ss], recv_sem=rg_r.at[slot],
            device_id={"domain": to}, device_id_type=MESHID)

    def products(p, panel):
        both = jnp.concatenate([pan[2 * panel], pan[2 * panel + 1]], axis=1)
        r = dot(wt[...], both)
        sbm[p] = r[0:128] + r[128:256]
        stripbuf[:, pl.ds(pl.multiple_of(panel * 256, 256), 256)] = r[256:288] + r[288:320]

    products(0, yh)
    for k in range(1, ND):
        to = lax.rem(d + k, ND)
        rm(0, to, d, k, to).start()

    for k in range(NCH):
        h = order(k)
        copy(part(across, h), part(across, h), bsem_s.at[h], bsem_r.at[h], y_peer).wait_recv()
        dcopy(h).start()
    for h in range(NCH):
        copy(part(mine, h), part(mine, h), dsem_s.at[h], dsem_r.at[h], c_peer).wait_recv()

    products(1, 1 - yh)
    for m in range(ND):
        sbg[8 * m:8 * m + 8, :] = stripbuf[8 * (m // 4):8 * (m // 4) + 8, 128 * (m % 4):128 * (m % 4) + 128]
    for k in range(1, ND):
        to = lax.rem(d + k, ND)
        rg(to, d, k, to).start()
    for k in range(1, ND):
        to = lax.rem(d + k, ND)
        rm(1, to, d, k, to).start()
    rsg[d] = sbg[rows(d), :]
    rsm[0, d] = sbm[0, rows(d), :]
    rsm[1, d] = sbm[1, rows(d), :]
    for k in range(1, ND):
        frm = lax.rem(d + k, ND)
        rg(frm, frm, k, frm).wait_recv()
    total = rsg[0]
    for m in range(1, ND):
        total = total + rsg[m]
    agg[rows(d), :] = total

    def ag(buf, who, ss, rr, k, to):
        view = buf.at[rows(who), :]
        return pltpu.make_async_remote_copy(
            src_ref=view, dst_ref=view, send_sem=ss.at[k], recv_sem=rr.at[who],
            device_id={"domain": to}, device_id_type=MESHID)

    for k in range(1, ND):
        to = lax.rem(d + k, ND)
        ag(agg, d, gg_s, gg_r, k, to).start()
    for p in range(2):
        for k in range(1, ND):
            frm = lax.rem(d + k, ND)
            rm(p, frm, frm, k, frm).wait_recv()
        total = rsm[p, 0]
        for m in range(1, ND):
            total = total + rsm[p, m]
        panel = yh if p == 0 else 1 - yh
        agm[rows(d), pl.ds(pl.multiple_of(panel * 256, 256), 256)] = total
    for k in range(1, ND):
        frm = lax.rem(d + k, ND)
        ag(agg, frm, gg_s, gg_r, k, frm).wait_recv()

    here = strip_of(band)
    gbuf[here] = agg[...]
    chip = band // 2

    def strip(who, ss, rr, k, to):
        return copy(gbuf.at[who], gbuf.at[who], ss.at[k], rr.at[who], to)

    for k in range(1, 8):
        to = lax.rem(chip + k, 8) * 2 + c
        strip(here, gx_s, gx_r, k, to).start()
    strip(here, gy_s, gy_r, 0, c_peer).start()
    for k in range(1, ND):
        to = lax.rem(d + k, ND)
        ag(agm, d, gm_s, gm_r, k, to).start()
    for k in range(1, 8):
        frm = strip_of(lax.rem(chip + k, 8) * 2 + c)
        strip(frm, gx_s, gx_r, k, c_peer).wait_recv()
        strip(frm, gy_s, gy_r, k, c_peer).start()
    for k in range(8):
        frm = strip_of(lax.rem(chip + k, 8) * 2 + (1 - c))
        strip(frm, gy_s, gy_r, k, c_peer).wait_recv()

    for b in range(16):
        for m in range(ND):
            ext[32 * b + 8 * (m // 4):32 * b + 8 * (m // 4) + 8, 128 * (m % 4):128 * (m % 4) + 128] = gbuf[b, 8 * m:8 * m + 8, :]

    factor(ext, inv)
    for k in range(1, ND):
        frm = lax.rem(d + k, ND)
        ag(agm, frm, gm_s, gm_r, k, frm).wait_recv()
    solve(ext, inv, agm, ybuf, zbuf, band)

    own = own_ref[0:OWNED, :]
    zh, zl = split2(zbuf[...])
    zz = jnp.concatenate([zh, zl], axis=0)
    pair = [jnp.concatenate([pan[0], pan[1]], axis=1), jnp.concatenate([pan[2], pan[3]], axis=1)]
    prod = nt(pair[0], zz[:, 0:256]) + nt(pair[1], zz[:, 256:512])
    update = prod[0:OWNED, 0:128] + prod[0:OWNED, 128:256]
    is_panel = band < 4
    zown = zbuf[:, pl.ds(pl.multiple_of(jnp.minimum(band, 3) * 128, 128), 128)]
    rest = (own - own.astype(bf16).astype(f32)).astype(bf16)
    fix = nt(rest, zown.astype(bf16))
    out_ref[...] = jnp.where(is_panel, -update - fix, own - update)

    @pl.when(x == 0)
    def _():
        for h in range(NCH):
            acopy(h, 0, y_peer).wait_send()
            acopy(h, 1, y_peer).wait_send()

    @pl.when((x == 1) | (x == 3))
    def _():
        for k in range(3):
            fcopy(0, k, y_peer).wait_send()

    for h in range(NCH):
        bcopy(h).wait_send()
        ccopy(h).wait_send()
        dcopy(h).wait_send()
    for k in range(1, ND):
        to = lax.rem(d + k, ND)
        rg(d, d, k, to).wait_send()
        rm(0, d, d, k, to).wait_send()
        rm(1, d, d, k, to).wait_send()
        ag(agg, d, gg_s, gg_r, k, to).wait_send()
        ag(agm, d, gm_s, gm_r, k, to).wait_send()
    for k in range(1, 8):
        strip(here, gx_s, gx_r, k, c_peer).wait_send()
    for k in range(8):
        strip(here, gy_s, gy_r, k, c_peer).wait_send()


def kernel(v_ref, pot_ref, mass_ref, mat_ref, conn_ref, face_ref, out_ref, own, wgt, vrecv, recv, pan, *scratch):
    d = lax.axis_index("domain")
    band = lax.axis_index("band")
    vrecv[...] = jnp.zeros(vrecv.shape, bf16)
    recv[...] = jnp.zeros(recv.shape, bf16)
    for j in range(4):
        pan[j, NCH * CH:ROWS, :] = jnp.zeros((ROWS - NCH * CH, COLS), bf16)
    barrier = pltpu.get_barrier_semaphore()
    for k in range(1, 16):
        pl.semaphore_signal(barrier, inc=1, device_id={"domain": lax.rem(d + k, ND)}, device_id_type=MESHID)
        pl.semaphore_signal(barrier, inc=1, device_id={"band": lax.rem(band + k, 16)}, device_id_type=MESHID)
    n = len(FILTER)
    f = scratch[:n]
    filter_states(d, lambda: pl.semaphore_wait(barrier, 30), v_ref, pot_ref, mass_ref, mat_ref, conn_ref, face_ref, own,
                  *f[:22], recv, f[22], vrecv, *f[23:], wgt)
    ortho(own, out_ref, d, band, wgt, pan, *scratch[n:])


V = pltpu.VMEM
D = pltpu.SemaphoreType.DMA
FILTER = (
    V((8, CS), f32), V((8, 256), f32), V((CS, 128), i32), V((256, 128), i32), V((ROWS, 128), f32),
    V((CP, CP), bf16), V((CS, CS), bf16), V((2 * FP, CS), bf16), V((CS, 512), bf16), V((ROWS, CS), bf16),
    V((ROWS, 256), bf16), V((CS, ROWS), bf16), V((ROWS, 512), bf16), V((CS, 128), f32), V((FP, 128), f32),
    V((CS, 128), f32), V((ROWS, 128), f32), V((2, CS, COLS), f32), V((CS, COLS), bf16), V((2, FP, COLS), f32),
    V((CS, COLS), f32),
    V((DEGREE, 2, FP, COLS), bf16), V((FP, COLS), bf16),
    D((DEGREE, 2)), D((DEGREE, 2)), D((2,)),
)
ORTHO = (
    V((320, ROWS), bf16), V((2, 128, 256), f32), V((2, ND, 8, 256), f32), V((128, 128), f32), V((ND, 8, 128), f32),
    V((128, 128), f32), V((128, 512), f32), V((16, 128, 128), f32), V((32, 512), f32), V((512, 512), f32), V((4, 128, 128), f32),
    V((128, 512), f32), V((128, 512), f32), V((ROWS, COLS), f32),
    D((2, NCH)), D((NCH,)), D((NCH,)), D((NCH,)), D((NCH,)), D((NCH,)), D((NCH,)), D((NCH,)), D((3,)),
    D((ND,)), D((ND,)), D((2, ND)), D((2, ND)), D((ND,)), D((ND,)), D((ND,)), D((ND,)), D((8,)), D((16,)), D((8,)), D((16,)),
)
SHARED = (V((ROWS, COLS), f32), V((ROWS, 128), f32), V((256, COLS), bf16), V((DEGREE, 512, COLS), bf16), V((4, ROWS, COLS), bf16))


def per_device(states, potential, node_mass, cell_matrix, connectivity, face_rows):
    return pl.pallas_call(
        kernel,
        out_shape=jax.ShapeDtypeStruct((OWNED, COLS), f32),
        in_specs=[VM] * 6,
        out_specs=VM,
        scratch_shapes=list(SHARED + FILTER + ORTHO),
        compiler_params=pltpu.CompilerParams(collective_id=0, has_side_effects=True, vmem_limit_bytes=60 << 20),
        name="subspace",
    )(states, potential.reshape(1, OWNED), node_mass.reshape(1, OWNED), cell_matrix, connectivity, face_rows)


def solution(mesh):
    return jax.shard_map(
        per_device, mesh=mesh,
        in_specs=(P("domain", "band"), P("domain"), P("domain"), P(), P("domain", None), P("domain", None)),
        out_specs=P("domain", "band"), check_vma=False,
    )
```

time: 166 us -> 118 us (0.71)
  Pallas kernels: 161 us -> 113 us
    pallas_call x2 -> x1, Pallas kernels: 161 us -> 113 us  [per_device(): pl.pallas_call(kernel, out_shape=jax.ShapeDtypeStruct((OWNED, COLS), f32)...]
where the time goes in v2:
time: 118 us
  Pallas kernels  113 us (96%)
  local copies, waits for them, and re-layouts  4.53 us (4%)
    pallas_call x1, Pallas kernels, per_device(): pl.pallas_call(kernel, out_shape=jax.ShapeDtypeStruct((OWNED, COLS), f32)...  113 us

profile of v2, /device:TPU:1, one launch (start us, length us, event | category | flops | bytes accessed | tf_op | source)
XLA Modules:
  0.0 117.9 jit_solution(14767442943505907512)
XLA Ops:
  0.0 1.3 %reshape.6.pot_ref = f32[1,1224]{1,0:T(1,128)} reshape(f32[1224]{0:T(1024)} %param.7) | data formatting | bytes 9792 | tf_op jit(solution)/shard_map/reshape | solution.py:582
  1.3 1.3 %reshape.7.mass_ref = f32[1,1224]{1,0:T(1,128)} reshape(f32[1224]{0:T(1024)} %param.8) | data formatting | bytes 9792 | tf_op jit(solution)/shard_map/reshape | solution.py:582
  2.6 113.4 %subspace.1 = f32[1224,128]{1,0:T(8,128)} custom-call(f32[1224,128]{1,0:T(8,128)} %v_ref.1, f32[1,1224]{1,0:T(1,128)} %reshape.6.pot_ref, f32[1,1224]{1,0:T(1,128)} %reshape.7.mass_ref, bf16[729,729]{1,0:T(8,128)(2,1)} %mat_ref.1, s32[2,729]{1,0:T(2,128)} %conn_ref.1, s32[1,153]{1,0:T(1,128)} %face_ref.1), custom_call_target="tpu_custom_call" | custom-call | tf_op jit(solution)/shard_map/subspace/pallas_call | solution.py:574
  116.0 1.9 %copy.8 = f32[1224,128]{1,0:T(8,128)} copy(f32[1224,128]{1,0:T(8,128)} %subspace.1) | data formatting | bytes 1253376

commit v3 on v2

--- a/solution.py
+++ b/solution.py
@@ -63,20 +63,31 @@
 
 
 def chol_inverse(block):
-    n = 128
+    n, groups = 128, 16
     shape = (8, n)
     lane = lanes(shape)
     sub = subs(shape)
-    a = [block[8 * k:8 * k + 8, :] for k in range(n // 8)]
+
+    def spread(x, j):
+        return jnp.broadcast_to(x[:, j:j + 1], shape)
+
+    def pick(x, i):
+        return jnp.take_along_axis(x, jnp.full(shape, i, i32), axis=0)
+
+    a = [block[8 * k:8 * k + 8, :] for k in range(groups)]
     out = []
-    for g in range(n // 8):
+    diag = [spread(a[0], q) for q in range(8)]
+    below = [spread(a[1], q) for q in range(8)]
+    ahead = [spread(a[1], 8 + q) for q in range(8)]
+    for g in range(groups):
         j0 = 8 * g
         inside = (lane >= j0) & (lane < j0 + 8)
-        here = a[g]
-        cols = [jnp.broadcast_to(here[:, j0 + k:j0 + k + 1], shape) for k in range(8)]
-        s = {(i, k): jnp.broadcast_to(cols[k][i:i + 1, :], shape) for k in range(8) for i in range(k, 8)}
-        r = [jnp.where(inside, 0.0, jnp.broadcast_to(here[i:i + 1, :], shape)) for i in range(8)]
-        inv, done = [], None
+        s = {(i, k): pick(diag[k], i) for k in range(8) for i in range(k, 8)}
+        r = [jnp.where(inside, 0.0, pick(a[g], i)) for i in range(8)]
+        near = range(g + 2, min(g + 4, groups))
+        side = {t: [spread(a[t], j0 + k) for k in range(8)] for t in near}
+        inv, done, mult = [], None, None
+        acc = jnp.where(inside, 0.0, a[g + 1]) if g + 1 < groups else None
         for k in range(8):
             root = lax.rsqrt(s[k, k])
             inv.append(root * root)
@@ -86,39 +97,59 @@
                 for q in range(k + 1, i + 1):
                     s[i, q] = s[i, q] - m * s[q, k]
                 r[i] = r[i] - m * r[k]
-            row = r[k] * root
+            if g + 1 < groups:
+                m = below[k] * inv[k]
+                for q in range(8):
+                    ahead[q] = ahead[q] - m * pick(below[k], q)
+                for q in range(k + 1, 8):
+                    below[q] = below[q] - m * s[q, k]
+                acc = acc - m * r[k]
+            row, part = r[k] * root, r[k] * inv[k]
             done = row if done is None else jnp.where(sub == k, row, done)
+            mult = part if mult is None else jnp.where(sub == k, part, mult)
         out.append(jnp.where(lane <= sub + j0, done, 0.0))
-        for t in range(g + 1, n // 8):
-            c = [jnp.broadcast_to(a[t][:, j0 + k:j0 + k + 1], shape) for k in range(8)]
-            acc = jnp.where(inside, 0.0, a[t])
+        if g + 1 < groups:
+            a[g + 1] = acc
+        for t in near:
+            c = side[t]
+            new = jnp.where(inside, 0.0, a[t])
             for k in range(8):
                 m = c[k] * inv[k]
                 for q in range(k + 1, 8):
                     c[q] = c[q] - m * s[q, k]
-                acc = acc - m * r[k]
-            a[t] = acc
+                new = new - m * r[k]
+            a[t] = new
+        if g + 4 < groups:
+            turned = mult.T
+            for t in range(g + 4, groups):
+                new = jnp.where(inside, 0.0, a[t])
+                for k in range(8):
+                    new = new - spread(turned[8 * t:8 * t + 8, :], k) * r[k]
+                a[t] = new
+        diag = ahead
+        if g + 2 < groups:
+            below = [spread(a[g + 2], j0 + 8 + q) for q in range(8)]
+            ahead = [spread(a[g + 2], j0 + 16 + q) for q in range(8)]
     return jnp.concatenate(out, axis=0)
 
 
-def factor(ext, inv):
+def factor(ext, inv, ybuf, arrive):
     for i in range(4):
         a, b = 128 * i, 128 * i + 128
         t = chol_inverse(ext[a:b, a:b])
         inv[i] = t
+        if i == 0:
+            arrive()
+        y = nt(ybuf[:, a:b], t, HIGH)
+        ybuf[:, a:b] = y
         if i < 3:
             low = nt(ext[b:512, a:b], t, HIGH)
             ext[b:512, a:b] = low
             ext[b:512, b:512] = ext[b:512, b:512] - nt(low, low, HIGH)
-
-
-def solve(ext, inv, m_ref, ybuf, zbuf, band):
-    for i in range(4):
-        a, b = 128 * i, 128 * i + 128
-        y = m_ref[:, a:b]
-        if i > 0:
-            y = y - nt(ybuf[:, 0:a], ext[a:b, 0:a], HIGH)
-        ybuf[:, a:b] = nt(y, inv[i], HIGH)
+            ybuf[:, b:512] = ybuf[:, b:512] - nt(y, low, HIGH)
+
+
+def solve(ext, inv, ybuf, zbuf, band):
     eye = jnp.where(lanes((128, 128)) == subs((128, 128)), 1.0, 0.0)
     for i in (3, 2, 1, 0):
         a, b = 128 * i, 128 * i + 128
@@ -129,6 +160,7 @@
 
 
 NCH = 6
+VLIM = 40 << 20
 CH = 208
 
 
@@ -221,15 +253,15 @@
         coef = jnp.where(t == 0, 0.125, 0.25).astype(f32)
         keep = jnp.where(t == 0, 0.0, 1.0).astype(f32)
         x = wb[...]
-        fc = dot(afac[...], x)
+        send[t, 0] = dot(afac[0:FP, :], x).astype(bf16)
+
+        @pl.when(d < ND - 1)
+        def _():
+            up(t, d + 1).start()
+
         wface = wf[now]
-        lower = fc[FP:2 * FP] + potf[...] * wface
-        send[t, 0] = fc[0:FP].astype(bf16)
+        lower = dot(afac[FP:2 * FP, :], x) + potf[...] * wface
         send[t, 1] = lower.astype(bf16)
-
-        @pl.when(d < ND - 1)
-        def _():
-            up(t, d + 1).start()
 
         @pl.when(d > 0)
         def _():
@@ -419,7 +451,7 @@
 
     products(1, 1 - yh)
     for m in range(ND):
-        sbg[8 * m:8 * m + 8, :] = stripbuf[8 * (m // 4):8 * (m // 4) + 8, 128 * (m % 4):128 * (m % 4) + 128]
+        sbg[8 * m:8 * m + 8, :] = stripbuf[8 * (m % 4):8 * (m % 4) + 8, 128 * (m // 4):128 * (m // 4) + 128]
     for k in range(1, ND):
         to = lax.rem(d + k, ND)
         rg(to, d, k, to).start()
@@ -463,33 +495,57 @@
     gbuf[here] = agg[...]
     chip = band // 2
 
-    def strip(who, ss, rr, k, to):
-        return copy(gbuf.at[who], gbuf.at[who], ss.at[k], rr.at[who], to)
+    def row_of(b):
+        return 2 * lax.rem(b // 2, 2) + b // 8
+
+    def strip(who, q, ss, rr, k, to):
+        view = gbuf.at[who, pl.ds(32 * q, 32), :]
+        return copy(view, view, ss.at[k, q], rr.at[who, q], to)
+
+    def blocks(b, act):
+        for q in range(4):
+            if q == 3:
+                act(q)
+            else:
+                pl.when(row_of(b) <= q)(functools.partial(act, q))
 
     for k in range(1, 8):
         to = lax.rem(chip + k, 8) * 2 + c
-        strip(here, gx_s, gx_r, k, to).start()
-    strip(here, gy_s, gy_r, 0, c_peer).start()
+        blocks(band, lambda q: strip(here, q, gx_s, gx_r, k, to).start())
+    blocks(band, lambda q: strip(here, q, gy_s, gy_r, 0, c_peer).start())
     for k in range(1, ND):
         to = lax.rem(d + k, ND)
         ag(agm, d, gm_s, gm_r, k, to).start()
     for k in range(1, 8):
-        frm = strip_of(lax.rem(chip + k, 8) * 2 + c)
-        strip(frm, gx_s, gx_r, k, c_peer).wait_recv()
-        strip(frm, gy_s, gy_r, k, c_peer).start()
+        who = lax.rem(chip + k, 8) * 2 + c
+        frm = strip_of(who)
+
+        def relay(q):
+            strip(frm, q, gx_s, gx_r, k, c_peer).wait_recv()
+            strip(frm, q, gy_s, gy_r, k, c_peer).start()
+
+        blocks(who, relay)
     for k in range(8):
-        frm = strip_of(lax.rem(chip + k, 8) * 2 + (1 - c))
-        strip(frm, gy_s, gy_r, k, c_peer).wait_recv()
+        who = lax.rem(chip + k, 8) * 2 + (1 - c)
+        frm = strip_of(who)
+        blocks(who, lambda q: strip(frm, q, gy_s, gy_r, k, c_peer).wait_recv())
 
     for b in range(16):
         for m in range(ND):
-            ext[32 * b + 8 * (m // 4):32 * b + 8 * (m // 4) + 8, 128 * (m % 4):128 * (m % 4) + 128] = gbuf[b, 8 * m:8 * m + 8, :]
-
-    factor(ext, inv)
-    for k in range(1, ND):
-        frm = lax.rem(d + k, ND)
-        ag(agm, frm, gm_s, gm_r, k, frm).wait_recv()
-    solve(ext, inv, agm, ybuf, zbuf, band)
+            if m // 4 >= b // 4:
+                ext[32 * b + 8 * (m % 4):32 * b + 8 * (m % 4) + 8, 128 * (m // 4):128 * (m // 4) + 128] = gbuf[b, 8 * m:8 * m + 8, :]
+    for i in range(3):
+        for j in range(i + 1, 4):
+            ext[128 * j:128 * j + 128, 128 * i:128 * i + 128] = ext[128 * i:128 * i + 128, 128 * j:128 * j + 128].T
+
+    def arrive():
+        for k in range(1, ND):
+            frm = lax.rem(d + k, ND)
+            ag(agm, frm, gm_s, gm_r, k, frm).wait_recv()
+        ybuf[...] = agm[...]
+
+    factor(ext, inv, ybuf, arrive)
+    solve(ext, inv, ybuf, zbuf, band)
 
     own = own_ref[0:OWNED, :]
     zh, zl = split2(zbuf[...])
@@ -526,14 +582,19 @@
         ag(agg, d, gg_s, gg_r, k, to).wait_send()
         ag(agm, d, gm_s, gm_r, k, to).wait_send()
     for k in range(1, 8):
-        strip(here, gx_s, gx_r, k, c_peer).wait_send()
-    for k in range(8):
-        strip(here, gy_s, gy_r, k, c_peer).wait_send()
-
-
-def kernel(v_ref, pot_ref, mass_ref, mat_ref, conn_ref, face_ref, out_ref, own, wgt, vrecv, recv, pan, *scratch):
+        blocks(band, lambda q: strip(here, q, gx_s, gx_r, k, c_peer).wait_send())
+    blocks(band, lambda q: strip(here, q, gy_s, gy_r, 0, c_peer).wait_send())
+    for k in range(1, 8):
+        blocks(lax.rem(chip + k, 8) * 2 + c, lambda q: strip(here, q, gy_s, gy_r, k, c_peer).wait_send())
+
+
+def kernel(v_hbm, pot_hbm, mass_hbm, mat_hbm, conn_hbm, face_hbm, out_ref, v_ref, pot_ref, mass_ref, mat_ref, conn_ref, face_ref, isem, own, wgt, vrecv, recv, pan, pot_row, mass_row, *scratch):
     d = lax.axis_index("domain")
     band = lax.axis_index("band")
+    loads = [pltpu.make_async_copy(src, dst, isem.at[k]) for k, (src, dst) in enumerate((
+        (face_hbm, face_ref), (pot_hbm, pot_ref), (v_hbm, v_ref), (conn_hbm, conn_ref), (mat_hbm, mat_ref), (mass_hbm, mass_ref)))]
+    for load in loads:
+        load.start()
     vrecv[...] = jnp.zeros(vrecv.shape, bf16)
     recv[...] = jnp.zeros(recv.shape, bf16)
     for j in range(4):
@@ -542,9 +603,19 @@
     for k in range(1, 16):
         pl.semaphore_signal(barrier, inc=1, device_id={"domain": lax.rem(d + k, ND)}, device_id_type=MESHID)
         pl.semaphore_signal(barrier, inc=1, device_id={"band": lax.rem(band + k, 16)}, device_id_type=MESHID)
+    for load in loads[:4]:
+        load.wait()
+    pot_row[...] = pot_ref[...].reshape(1, OWNED)
     n = len(FILTER)
     f = scratch[:n]
-    filter_states(d, lambda: pl.semaphore_wait(barrier, 30), v_ref, pot_ref, mass_ref, mat_ref, conn_ref, face_ref, own,
+
+    def barrier_wait():
+        pl.semaphore_wait(barrier, 30)
+        loads[4].wait()
+        loads[5].wait()
+        mass_row[...] = mass_ref[...].reshape(1, OWNED)
+
+    filter_states(d, barrier_wait, v_ref, pot_row, mass_row, mat_ref, conn_ref, face_ref, own,
                   *f[:22], recv, f[22], vrecv, *f[23:], wgt)
     ortho(own, out_ref, d, band, wgt, pan, *scratch[n:])
 
@@ -565,21 +636,22 @@
     V((128, 128), f32), V((128, 512), f32), V((16, 128, 128), f32), V((32, 512), f32), V((512, 512), f32), V((4, 128, 128), f32),
     V((128, 512), f32), V((128, 512), f32), V((ROWS, COLS), f32),
     D((2, NCH)), D((NCH,)), D((NCH,)), D((NCH,)), D((NCH,)), D((NCH,)), D((NCH,)), D((NCH,)), D((3,)),
-    D((ND,)), D((ND,)), D((2, ND)), D((2, ND)), D((ND,)), D((ND,)), D((ND,)), D((ND,)), D((8,)), D((16,)), D((8,)), D((16,)),
+    D((ND,)), D((ND,)), D((2, ND)), D((2, ND)), D((ND,)), D((ND,)), D((ND,)), D((ND,)), D((8, 4)), D((16, 4)), D((8, 4)), D((16, 4)),
 )
-SHARED = (V((ROWS, COLS), f32), V((ROWS, 128), f32), V((256, COLS), bf16), V((DEGREE, 512, COLS), bf16), V((4, ROWS, COLS), bf16))
+SHARED = (V((OWNED, COLS), f32), V((OWNED,), f32), V((OWNED,), f32), V((CELL, CELL), bf16), V((2, CELL), i32), V((1, FACE), i32), D((6,)),
+          V((ROWS, COLS), f32), V((ROWS, 128), f32), V((256, COLS), bf16), V((DEGREE, 512, COLS), bf16), V((4, ROWS, COLS), bf16), V((1, OWNED), f32), V((1, OWNED), f32))
 
 
 def per_device(states, potential, node_mass, cell_matrix, connectivity, face_rows):
     return pl.pallas_call(
         kernel,
         out_shape=jax.ShapeDtypeStruct((OWNED, COLS), f32),
-        in_specs=[VM] * 6,
+        in_specs=[pl.BlockSpec(memory_space=pltpu.HBM)] * 6,
         out_specs=VM,
         scratch_shapes=list(SHARED + FILTER + ORTHO),
-        compiler_params=pltpu.CompilerParams(collective_id=0, has_side_effects=True, vmem_limit_bytes=60 << 20),
+        compiler_params=pltpu.CompilerParams(collective_id=0, has_side_effects=True, vmem_limit_bytes=VLIM),
         name="subspace",
-    )(states, potential.reshape(1, OWNED), node_mass.reshape(1, OWNED), cell_matrix, connectivity, face_rows)
+    )(states, potential, node_mass, cell_matrix, connectivity, face_rows)
 
 
 def solution(mesh):

time: 118 us -> 112 us (0.949)
  Pallas kernels: 113 us -> 106 us
  local copies, waits for them, and re-layouts: 4.53 us -> 5.92 us
    pallas_call x1, Pallas kernels: 113 us -> 106 us  [per_device(): pl.pallas_call(kernel, out_shape=jax.ShapeDtypeStruct((OWNED, COLS), f32)...]
    unnamed x1 -> x13, local copies, waits for them, and re-layouts: 1.95 us -> 5.92 us
    reshape x2 -> x0, local copies, waits for them, and re-layouts: 2.59 us -> none  [the longest x1 1.29 us: per_device(): node_mass.reshape(1, OWNED)]
where the time goes in v3:
time: 112 us
  Pallas kernels  106 us (95%)
  local copies, waits for them, and re-layouts  5.92 us (5%)
    pallas_call x1, Pallas kernels, per_device(): pl.pallas_call(kernel, out_shape=jax.ShapeDtypeStruct((OWNED, COLS), f32)...  106 us
    unnamed x13, local copies, waits for them, and re-layouts  5.92 us

profile of v3, /device:TPU:1, one launch (start us, length us, event | category | flops | bytes accessed | tf_op | source)
XLA Modules:
  0.0 112.2 jit_solution(283850776593676430)
XLA Ops:
  0.0 0.0 copy-start
  0.0 1.3 %copy-done = bf16[729,729]{1,0:T(8,128)(2,1)S(1)} copy-done((bf16[729,729]{1,0:T(8,128)(2,1)S(1)}, bf16[729,729]{1,0:T(8,128)(2,1)}, u32[]{:S(2)}) %copy-start) | copy-done | bytes 1062906
  1.3 0.0 copy-start.1
  1.3 1.1 copy-done.1
  2.3 0.0 copy-start.2
  2.3 0.7 copy-done.2
  3.0 0.0 copy-start.3
  3.0 0.7 copy-done.3
  3.7 0.0 copy-start.4
  3.7 0.7 copy-done.4
  4.4 0.0 copy-start.5
  4.4 0.7 copy-done.5
  5.1 106.2 %subspace.1 = f32[1224,128]{1,0:T(8,128)S(1)} custom-call(f32[1224,128]{1,0:T(8,128)S(1)} %copy-done.1, f32[1224]{0:T(1024)S(1)} %copy-done.2, f32[1224]{0:T(1024)S(1)} %copy-done.3, bf16[729,729]{1,0:T(8,128)(2,1)S(1)} %copy-done, s32[2,729]{1,0:T(2,128)S(1)} %copy-done.4, s32[1,153]{1,0:T(1,128)S(1)} %copy-done.5), custom_call_target="tpu_custom_call" | custom-call | tf_op jit(solution)/shard_map/subspace/pallas_call | solution.py:646
  111.3 0.8 copy.8
Async XLA Ops:
  0.0 1.3 %copy-start = (bf16[729,729]{1,0:T(8,128)(2,1)S(1)}, bf16[729,729]{1,0:T(8,128)(2,1)}, u32[]{:S(2)}) copy-start(bf16[729,729]{1,0:T(8,128)(2,1)} %mat_hbm.1) | copy-start | bytes 3188650
  1.3 1.1 copy-start.1
  2.3 0.7 copy-start.2
  3.0 0.7 copy-start.3
  3.7 0.7 copy-start.4
  4.4 0.7 copy-start.5

commit v4 on v3

--- a/solution.py
+++ b/solution.py
@@ -133,20 +133,39 @@
     return jnp.concatenate(out, axis=0)
 
 
+def nt3(a, b):
+    ah, al = split2(a)
+    bh, bl = split2(b)
+    return nt(jnp.concatenate([ah, ah, al], axis=1), jnp.concatenate([bh, bl, bh], axis=1))
+
+
+def nn3(a, b):
+    ah, al = split2(a)
+    bh, bl = split2(b)
+    return dot(jnp.concatenate([ah, ah, al], axis=1), jnp.concatenate([bh, bl, bh], axis=0))
+
+
 def factor(ext, inv, ybuf, arrive):
+    def forward(i):
+        a, b = 128 * i, 128 * i + 128
+        y = nt3(ybuf[:, a:b], inv[i])
+        ybuf[:, a:b] = y
+        if i < 3:
+            ybuf[:, b:512] = ybuf[:, b:512] - nt3(y, ext[b:512, a:b])
+
     for i in range(4):
         a, b = 128 * i, 128 * i + 128
         t = chol_inverse(ext[a:b, a:b])
         inv[i] = t
-        if i == 0:
+        if i < 3:
+            low = nt3(ext[b:512, a:b], t)
+            ext[b:512, a:b] = low
+            ext[b:512, b:512] = ext[b:512, b:512] - nt3(low, low)
+        if i == 1:
             arrive()
-        y = nt(ybuf[:, a:b], t, HIGH)
-        ybuf[:, a:b] = y
-        if i < 3:
-            low = nt(ext[b:512, a:b], t, HIGH)
-            ext[b:512, a:b] = low
-            ext[b:512, b:512] = ext[b:512, b:512] - nt(low, low, HIGH)
-            ybuf[:, b:512] = ybuf[:, b:512] - nt(y, low, HIGH)
+            forward(0)
+        if i > 0:
+            forward(i)
 
 
 def solve(ext, inv, ybuf, zbuf, band):
@@ -155,12 +174,12 @@
         a, b = 128 * i, 128 * i + 128
         y = jnp.where(band < 4, jnp.where(band == i, -eye, 0.0), ybuf[:, a:b])
         if i < 3:
-            y = y - nn(zbuf[:, b:512], ext[b:512, a:b])
-        zbuf[:, a:b] = nn(y, inv[i])
+            y = y - nn3(zbuf[:, b:512], ext[b:512, a:b])
+        zbuf[:, a:b] = nn3(y, inv[i])
 
 
 NCH = 6
-VLIM = 40 << 20
+VLIM = 60 << 20
 CH = 208
 
 
@@ -280,7 +299,7 @@
             e10 = jnp.where(c1 >= 0, onehot(c1 == crow[0:1, 0:CP].astype(i32)), none)
             amat[CP:CS, 0:CP] = dot(e10, km).astype(bf16)
 
-        ybuf[...] = dot(amat[...], x)
+        ybuf[...] = coef * (dot(amat[...], x) * msk[...] + (potc[...] - 9.0) * ws[now]) - keep * ws[then]
 
         @pl.when(t < 5)
         def _():
@@ -303,17 +322,14 @@
         @pl.when(d > 0)
         def _():
             up(t, d).wait_recv()
-            down(t, d).wait_send()
 
         @pl.when(d < ND - 1)
         def _():
             down(t, d).wait_recv()
-            up(t, d).wait_send()
 
         got = recv[t]
         wf[then] = coef * (lower + got[0:FP].astype(f32) - 9.0 * wface) - keep * wf[then]
-        total = (ybuf[...] + dot(bmat[...], got)) * msk[...]
-        new = coef * (total + (potc[...] - 9.0) * ws[now]) - keep * ws[then]
+        new = ybuf[...] + coef * dot(bmat[...], got)
         ws[then] = new
         wb[...] = new.astype(bf16)
         return carry
@@ -323,6 +339,13 @@
     @pl.when(d > 0)
     def _():
         vcopy(d).wait_send()
+        for t in range(DEGREE):
+            down(t, d).wait_send()
+
+    @pl.when(d < ND - 1)
+    def _():
+        for t in range(DEGREE):
+            up(t, d).wait_send()
 
     hi, lo = split2(ws[DEGREE % 2])
     back = dot(gt[...], jnp.concatenate([hi, lo], axis=1))
@@ -478,6 +501,32 @@
     for k in range(1, ND):
         to = lax.rem(d + k, ND)
         ag(agg, d, gg_s, gg_r, k, to).start()
+    for k in range(1, ND):
+        frm = lax.rem(d + k, ND)
+        ag(agg, frm, gg_s, gg_r, k, frm).wait_recv()
+
+    here = strip_of(band)
+    gbuf[here] = agg[...]
+    chip = band // 2
+
+    def row_of(b):
+        return 2 * lax.rem(b // 2, 2) + b // 8
+
+    def strip(who, q, ss, rr, k, to):
+        view = gbuf.at[who, pl.ds(32 * q, 32), :]
+        return copy(view, view, ss.at[k, q], rr.at[who, q], to)
+
+    def blocks(b, act):
+        for q in range(4):
+            if q == 3:
+                act(q)
+            else:
+                pl.when(row_of(b) <= q)(functools.partial(act, q))
+
+    for k in range(1, 8):
+        to = lax.rem(chip + k, 8) * 2 + c
+        blocks(band, lambda q: strip(here, q, gx_s, gx_r, k, to).start())
+    blocks(band, lambda q: strip(here, q, gy_s, gy_r, 0, c_peer).start())
     for p in range(2):
         for k in range(1, ND):
             frm = lax.rem(d + k, ND)
@@ -487,32 +536,6 @@
             total = total + rsm[p, m]
         panel = yh if p == 0 else 1 - yh
         agm[rows(d), pl.ds(pl.multiple_of(panel * 256, 256), 256)] = total
-    for k in range(1, ND):
-        frm = lax.rem(d + k, ND)
-        ag(agg, frm, gg_s, gg_r, k, frm).wait_recv()
-
-    here = strip_of(band)
-    gbuf[here] = agg[...]
-    chip = band // 2
-
-    def row_of(b):
-        return 2 * lax.rem(b // 2, 2) + b // 8
-
-    def strip(who, q, ss, rr, k, to):
-        view = gbuf.at[who, pl.ds(32 * q, 32), :]
-        return copy(view, view, ss.at[k, q], rr.at[who, q], to)
-
-    def blocks(b, act):
-        for q in range(4):
-            if q == 3:
-                act(q)
-            else:
-                pl.when(row_of(b) <= q)(functools.partial(act, q))
-
-    for k in range(1, 8):
-        to = lax.rem(chip + k, 8) * 2 + c
-        blocks(band, lambda q: strip(here, q, gx_s, gx_r, k, to).start())
-    blocks(band, lambda q: strip(here, q, gy_s, gy_r, 0, c_peer).start())
     for k in range(1, ND):
         to = lax.rem(d + k, ND)
         ag(agm, d, gm_s, gm_r, k, to).start()

time: 112 us -> 109 us (0.973)
  local copies, waits for them, and re-layouts: 5.92 us -> 1.95 us
    unnamed x13 -> x1, local copies, waits for them, and re-layouts: 5.92 us -> 1.95 us
where the time goes in v4:
time: 109 us; the launch traced here: 108 us
  Pallas kernels  106 us (97%)
  local copies, waits for them, and re-layouts  1.95 us (2%)
    pallas_call x1, Pallas kernels, per_device(): pl.pallas_call(kernel, out_shape=jax.ShapeDtypeStruct((OWNED, COLS), f32)...  106 us

profile of v4, /device:TPU:1, one launch (start us, length us, event | category | flops | bytes accessed | tf_op | source)
XLA Modules:
  0.0 108.4 jit_solution(9219616573848381313)
XLA Ops:
  0.0 106.5 %subspace.1 = f32[1224,128]{1,0:T(8,128)} custom-call(f32[1224,128]{1,0:T(8,128)} %v_hbm.1, f32[1224]{0:T(1024)} %pot_hbm.1, f32[1224]{0:T(1024)} %mass_hbm.1, bf16[729,729]{1,0:T(8,128)(2,1)} %mat_hbm.1, s32[2,729]{1,0:T(2,128)} %conn_hbm.1, s32[1,153]{1,0:T(1,128)} %face_hbm.1), custom_call_target="tpu_custom_call" | custom-call | tf_op jit(solution)/shard_map/subspace/pallas_call | solution.py:669
  106.5 1.9 %copy.8 = f32[1224,128]{1,0:T(8,128)} copy(f32[1224,128]{1,0:T(8,128)} %subspace.1) | data formatting | bytes 1253376

commit v5 on v4

--- a/solution.py
+++ b/solution.py
@@ -120,12 +120,13 @@
                 new = new - m * r[k]
             a[t] = new
         if g + 4 < groups:
-            turned = mult.T
+            t0 = 8 * (g + 4)
+            full = None
+            for i in range(8):
+                full = r[i] if full is None else jnp.where(sub == i, r[i], full)
+            far = jnp.dot(mult.T[t0:n, :], full, preferred_element_type=f32, precision=HIGH)
             for t in range(g + 4, groups):
-                new = jnp.where(inside, 0.0, a[t])
-                for k in range(8):
-                    new = new - spread(turned[8 * t:8 * t + 8, :], k) * r[k]
-                a[t] = new
+                a[t] = jnp.where(inside, 0.0, a[t]) - far[8 * t - t0:8 * t - t0 + 8, :]
         diag = ahead
         if g + 2 < groups:
             below = [spread(a[g + 2], j0 + 8 + q) for q in range(8)]
@@ -241,13 +242,10 @@
         afac[:, cols] = dot(both[:, cols], kp[...]).astype(bf16)
     for t in range(ROWS // 128):
         gsel[:, 128 * t:128 * t + 128] = onehot(connb[...] == lanes((CS, 128), 128 * t))
-    cv = dot(gsel[...], v3[...])
+    cv = dot(gsel[...], v3[:, 0:256])
     ws[0] = cv[:, 0:128] + cv[:, 128:256]
-    potc[...] = cv[:, 256:384] + cv[:, 384:512]
     cb2 = jnp.tile(connb[...], (1, 2))
-    bmat[:, 0:256] = onehot(cb2 == fi)
     bmat[:, 256:512] = onehot(cb2 == lanes((CS, 256), OWNED))
-    msk[...] = jnp.where((connb[...] >= OWNED) & (d == ND - 1), 0.0, 1.0)
 
     @pl.when(d < ND - 1)
     def _():
@@ -298,6 +296,10 @@
             c1 = jnp.tile(connb[CP:CS, :], (1, CP // 128))
             e10 = jnp.where(c1 >= 0, onehot(c1 == crow[0:1, 0:CP].astype(i32)), none)
             amat[CP:CS, 0:CP] = dot(e10, km).astype(bf16)
+            cp = dot(gsel[...], v3[:, 256:512])
+            potc[...] = cp[:, 0:128] + cp[:, 128:256]
+            bmat[:, 0:256] = onehot(jnp.tile(connb[...], (1, 2)) == fi)
+            msk[...] = jnp.where((connb[...] >= OWNED) & (d == ND - 1), 0.0, 1.0)
 
         ybuf[...] = coef * (dot(amat[...], x) * msk[...] + (potc[...] - 9.0) * ws[now]) - keep * ws[then]
 

time: 109 us -> 105 us (0.963)
  Pallas kernels: 106 us -> 103 us
    pallas_call x1, Pallas kernels: 106 us -> 103 us  [per_device(): pl.pallas_call(kernel, out_shape=jax.ShapeDtypeStruct((OWNED, COLS), f32)...]
where the time goes in v5:
time: 105 us
  Pallas kernels  103 us (98%)
  local copies, waits for them, and re-layouts  1.95 us (2%)
    pallas_call x1, Pallas kernels, per_device(): pl.pallas_call(kernel, out_shape=jax.ShapeDtypeStruct((OWNED, COLS), f32)...  103 us

profile of v5, /device:TPU:1, one launch (start us, length us, event | category | flops | bytes accessed | tf_op | source)
XLA Modules:
  0.0 104.9 jit_solution(1097063351935450099)
XLA Ops:
  0.0 102.9 %subspace.1 = f32[1224,128]{1,0:T(8,128)} custom-call(f32[1224,128]{1,0:T(8,128)} %v_hbm.1, f32[1224]{0:T(1024)} %pot_hbm.1, f32[1224]{0:T(1024)} %mass_hbm.1, bf16[729,729]{1,0:T(8,128)(2,1)} %mat_hbm.1, s32[2,729]{1,0:T(2,128)} %conn_hbm.1, s32[1,153]{1,0:T(1,128)} %face_hbm.1), custom_call_target="tpu_custom_call" | custom-call | tf_op jit(solution)/shard_map/subspace/pallas_call | solution.py:671
  102.9 1.9 %copy.8 = f32[1224,128]{1,0:T(8,128)} copy(f32[1224,128]{1,0:T(8,128)} %subspace.1) | data formatting | bytes 1253376
